TPU v7x, 128 devices: a whole 4x4x4 slice. The times are simulated.
128 devices in a mesh: member: 4 (over z), tile: 32 (over y, x, core).
Axes of the slice: x: 4, y: 4, z: 4, core: 2. Of those that a mesh axis runs over, the one named last changes fastest.
Arguments:
- teacher_logits: bfloat16 [16, 4096, 4096], P('member', 'tile'), may hold values from -8 to 260
- coverage: int32 [4096], P('tile'), may hold values from 0 to 31, as said below
- features: bfloat16 [4, 1024, 64, 256], P('member', 'tile'), may hold values from -6 to 6
- labels: int32 [4, 1024, 64], P('member', 'tile'), may hold values from 0 to 63
- first_weight: bfloat16 [3, 3, 256, 256], replicated, may hold values from -0.125 to 0.125
- second_weight: bfloat16 [3, 3, 256, 256], replicated, may hold values from -0.125 to 0.125
- head_weight: bfloat16 [256, 64], replicated, may hold values from -0.375 to 0.375
Outputs:
- first_kernel_grad: float32 [3, 3, 256, 256], replicated
- second_kernel_grad: float32 [3, 3, 256, 256], replicated
- head_kernel_grad: float32 [256, 64], replicated
- loss_value: float32 [], replicated
Inputs may be any that keep to these rules, and one draw needn't show every extreme that they name: Slot k of column t goes to column coverage[t * 128 + k]; for every slot each column receives it from exactly one column. Within each block of 32 consecutive slots a column sends at most 2 tiles to any one column and exactly 2 to one; over all 128 slots at most 8 to any one column, reached.
All inputs are finite; a program needn't handle non-finite values.
Results may differ from a plain program's by a relative error of at most 0.013.
The roundings to bfloat16 on the way count: a program that leaves them out, or rounds other values in their place, can miss the bound.
Values may be sent and summed in bfloat16 or wider, within the bound.
A program may use at most 128 MiB of HBM per device.

v0:
```python
import math

import jax
import jax.numpy as jnp
from jax import lax
from jax.experimental import pallas as pl
from jax.experimental.pallas import tpu as pltpu
from jax.sharding import PartitionSpec as P

F32 = jnp.float32
BF16 = jnp.bfloat16
I32 = jnp.int32
MESH = pl.DeviceIdType.MESH

CH = 256
NCLS = 64
NZ = 4
NT = 32
ROWS = 32
COLS = 64
CELLS = ROWS * COLS
NSEM = 200


def iota(shape, dim):
    return lax.broadcasted_iota(I32, shape, dim)


def onehot(mask):
    return jnp.where(mask, 1.0, 0.0).astype(BF16)


def mm(a, b):
    return jnp.dot(a, b, preferred_element_type=F32)


def mm_dims(a, b, ca, cb):
    return lax.dot_general(a, b, (((ca,), (cb,)), ((), ())), preferred_element_type=F32)


def kernel(
    tl, cov, feat, lab, w1h, w2h, wh,
    o1, o2, ohead, oloss,
    tv, xb, a1, a1e, a1o, a2, a2t, ag, gp, w1, w2, w2t,
    hf, gf, df, gat,
    rel_s, rel_r, fin_s, fin_l, fin_r, own, part, sec_s, sec_r,
    mp, sb, rb, mean_t,
    csb, crb, acc, s1b, r1, a1c, s2b, r2, x3,
    hx, lx,
    ssem, rsem, lsem,
):
    z = lax.axis_index("member")
    t = lax.axis_index("tile")
    core = lax.rem(t, 2)
    xc = lax.rem(lax.div(t, 2), 4)
    yc = lax.div(t, 8)
    coords = {"x": xc, "y": yc, "z": z, "c": core}

    def peer(axis, j):
        if axis == "z":
            return (j, t)
        if axis == "x":
            return (z, yc * 8 + j * 2 + core)
        if axis == "y":
            return (z, j * 8 + xc * 2 + core)
        return (z, yc * 8 + xc * 2 + j)

    used = [0]
    sent = []

    def remote(src, dst, dev):
        i = used[0]
        used[0] += 1
        copy = pltpu.make_async_remote_copy(
            src_ref=src, dst_ref=dst, send_sem=ssem.at[i], recv_sem=rsem.at[i],
            device_id=dev, device_id_type=MESH,
        )
        copy.start()
        sent.append(copy)
        return copy

    def ring(axis, o):
        return lax.rem(coords[axis] + o, 4)

    barrier = pltpu.get_barrier_semaphore()
    for o in range(1, NT):
        pl.semaphore_signal(barrier, inc=1, device_id=(z, lax.rem(t + o, NT)), device_id_type=MESH)
    for o in range(1, NZ):
        pl.semaphore_signal(barrier, inc=1, device_id=(lax.rem(z + o, NZ), t), device_id_type=MESH)

    zr, zl, zf = lax.rem(z + 1, NZ), lax.rem(z + 3, NZ), lax.rem(z + 2, NZ)
    loads = []
    for ci, g in enumerate((zf, zr, zl, z)):
        c = pltpu.make_async_copy(
            tl.at[:, pl.ds(pl.multiple_of(g * 32, 32), 32), :], tv.at[ci], lsem.at[ci]
        )
        c.start()
        loads.append(c)
    load_x = pltpu.make_async_copy(feat, xb.at[pl.ds(192, CELLS), :], lsem.at[4])
    load_w1 = pltpu.make_async_copy(w1h, w1, lsem.at[5])
    load_w2 = pltpu.make_async_copy(w2h, w2, lsem.at[6])
    load_x.start()
    load_w1.start()
    load_w2.start()

    group = onehot(lax.div(iota((256, 256), 0), 64) == lax.div(iota((256, 256), 1), 64))
    squash = onehot(lax.div(iota((256, 128), 0), 64) == iota((256, 128), 1))

    def cell_sum(v):
        hi = v.astype(BF16)
        lo = (v - hi.astype(F32)).astype(BF16)
        both = mm(jnp.concatenate([hi, lo], axis=0), squash)
        return both[:32] + both[32:]

    def soft(ci, half, put, sec):
        def step(k, sec):
            lane = pl.multiple_of(half * 2048 + k * 256, 256)
            x = tv[ci, :, :, pl.ds(lane, 256)].reshape(128, 256).astype(F32)
            e4 = jnp.exp2(x * (math.log2(math.e) / 4.0))
            r = e4 / mm(e4.astype(BF16), group)
            r2 = r * r
            e = (r2 * r2).astype(BF16)
            p = e.astype(F32) / mm(e, group)
            p = p.reshape(4, 32, 256)
            sq = p * p
            put(k, (p[0] + p[1]) + (p[2] + p[3]))
            q = (sq[0] + sq[1]) + (sq[2] + sq[3])
            return sec + pltpu.roll(cell_sum(q), half * 32 + 4 * k, 1)

        return lax.fori_loop(0, 8, step, sec)

    def at(k):
        return pl.ds(pl.multiple_of(k * 256, 256), 256)

    def put_to(ref, *lead):
        def put(k, v):
            ref[(*lead, slice(None), at(k))] = v.astype(ref.dtype)

        return put

    zero_sec = jnp.zeros((32, 128), F32)
    loads[0].wait()
    sec_f = soft(0, 0, put_to(rel_s, 0), zero_sec)
    pl.semaphore_wait(barrier, NT - 1 + NZ - 1)
    relay_a = remote(rel_s.at[0], rel_r.at[0], (zr, t))
    up, down = lax.rem(t + 1, NT), lax.rem(t + NT - 1, NT)
    halo_up = remote(feat.at[pl.ds(CELLS - 192, 192), :], xb.at[pl.ds(0, 192), :], (z, up))
    halo_dn = remote(feat.at[pl.ds(0, 192), :], xb.at[pl.ds(192 + CELLS, 192), :], (z, down))
    sec_f = soft(0, 1, put_to(rel_s, 1), sec_f)
    relay_b = remote(rel_s.at[1], rel_r.at[1], (zl, t))
    sec_s[0] = sec_f
    sec_c = [remote(sec_s.at[0], sec_r.at[0], (zf, t))]
    loads[1].wait()
    sec_1 = soft(1, 1, put_to(fin_s, 0, 1), zero_sec)
    f0 = remote(fin_s.at[0, 1], fin_l.at[1], (zr, t))
    loads[2].wait()
    sec_2 = soft(2, 0, put_to(fin_s, 1, 0), zero_sec)
    f1 = remote(fin_s.at[1, 0], fin_r.at[0], (zl, t))
    sec_1 = soft(1, 0, put_to(part), sec_1)
    sec_s[1] = sec_1
    sec_c.append(remote(sec_s.at[1], sec_r.at[1], (zr, t)))

    def add_relay(side, half):
        def step(k, carry):
            fin_s[side, half, :, at(k)] = (
                part[:, at(k)] + rel_r[half, :, at(k)].astype(F32)
            ).astype(BF16)
            return carry

        lax.fori_loop(0, 8, step, 0)

    relay_a.wait_recv()
    add_relay(0, 0)
    f2 = remote(fin_s.at[0, 0], fin_l.at[0], (zr, t))
    sec_2 = soft(2, 1, put_to(part), sec_2)
    sec_s[2] = sec_2
    sec_c.append(remote(sec_s.at[2], sec_r.at[2], (zl, t)))
    relay_b.wait_recv()
    add_relay(1, 1)
    f3 = remote(fin_s.at[1, 1], fin_r.at[1], (zl, t))
    loads[3].wait()
    sec_m = soft(3, 0, put_to(own, 0), zero_sec)
    sec_m = soft(3, 1, put_to(own, 1), sec_m)

    def shifted(v, by, lo_col, hi_col, rows):
        col = lax.rem(iota((rows, CH), 0), COLS)
        before = jnp.where(col >= by, pltpu.roll(v, by, 0), 0.0)
        after = jnp.where(col < COLS - by, pltpu.roll(v, rows - by, 0), 0.0)
        return before.astype(BF16), after.astype(BF16)

    load_x.wait()
    load_w1.wait()
    halo_up.wait_recv()
    halo_dn.wait_recv()

    def build_one(k, carry):
        s = pl.ds(pl.multiple_of(k * 128, 128), 128)
        row = t * ROWS - 3 + 2 * k + lax.div(iota((128, CH), 0), COLS)
        v = xb[s, :].astype(F32)
        v = jnp.where((row >= 0) & (row < NT * ROWS), v, 0.0)
        before, after = shifted(v, 1, 0, 0, 128)
        a1[s, 0:CH] = before
        a1[s, CH:2 * CH] = v.astype(BF16)
        a1[s, 2 * CH:3 * CH] = after
        return carry

    lax.fori_loop(0, 19, build_one, 0)

    def conv_rows(a_ref, w_ref, start, rows, stride):
        total = None
        for a in range(3):
            s = pl.ds(pl.multiple_of(start + a * stride, 64), rows)
            d = mm(a_ref[s, :], w_ref[a])
            total = d if total is None else total + d
        return total

    def conv_one(k, carry):
        n = 256
        start = k * n
        pre = conv_rows(a1, w1, start, n, COLS)
        row = t * ROWS - 2 + 4 * k + lax.div(iota((n, CH), 0), COLS)
        h = jnp.where((row >= 0) & (row < NT * ROWS) & (pre > 0), pre, 0.0)
        h = h.astype(BF16).astype(F32)
        before, after = shifted(h, 2, 0, 0, n)
        s = pl.ds(pl.multiple_of(start, n), n)
        a2[s, 0:CH] = before
        a2[s, CH:2 * CH] = h.astype(BF16)
        a2[s, 2 * CH:3 * CH] = after
        return carry

    lax.fori_loop(0, 9, conv_one, 0)

    for c in (f0, f1, f2, f3, *sec_c):
        c.wait_recv()

    msq = zero_sec
    for half in range(2):
        def mean_step(k, msq, half=half):
            for sub in range(2):
                s = pl.ds(pl.multiple_of(k * 512 + sub * 256, 256), 256)
                m = (
                    own[half, :, s] + fin_l[half, :, s].astype(F32) + fin_r[half, :, s].astype(F32)
                ) * (1.0 / 16.0)
                mp[pl.ds(pl.multiple_of((half * 4 + k) * 32, 32), 32), sub * 256:(sub + 1) * 256] = (
                    m.astype(BF16)
                )
                msq = msq + pltpu.roll(cell_sum(m * m), half * 32 + 8 * k + 4 * sub, 1)
            return msq

        msq = lax.fori_loop(0, 4, mean_step, msq)
    second = (sec_m + sec_r[0]) + (sec_r[1] + sec_r[2])
    spread = second * (1.0 / 16.0) - msq
    lane = iota((32, 128), 1)
    slot_no = (iota((32, 128), 0) + 1).astype(F32)
    for a in range(8):
        sp = spread if a == 0 else pltpu.roll(spread, 128 - 8 * a, 1)
        sp = jnp.where(lane < 8, sp, 0.0)
        hi = sp.astype(BF16).astype(F32)
        mid = (sp - hi).astype(BF16).astype(F32)
        lo = sp - hi - mid
        ext = hi + pltpu.roll(mid, 8, 1) + pltpu.roll(lo, 16, 1)
        ext = jnp.where(lane == 24, slot_no, ext)
        mp[a * 32:(a + 1) * 32, 512:640] = ext.astype(BF16)

    crow = cov[...]
    i0, i1 = iota((128, 128), 0), iota((128, 128), 1)
    ccol = jnp.sum(jnp.where(i0 == i1, crow, 0), axis=1, keepdims=True)
    same = (ccol == crow) & (lax.div(i0, 32) == lax.div(i1, 32)) & (i0 < i1)
    rank = jnp.sum(jnp.where(same, 1, 0), axis=0, keepdims=True)
    slot = jnp.broadcast_to(crow * 2 + rank, (8, 128)).astype(F32)
    lane8 = iota((8, 128), 1)
    mine = jnp.zeros((8, 128), F32)
    for g in range(NZ):
        moved = slot if g == 0 else pltpu.roll(slot, 128 - 32 * g, 1)
        mine = jnp.where(z == g, moved, mine)
    mine = jnp.where(lane8 < 32, mine, 0.0)
    mine = mine + pltpu.roll(mine, 32, 1)
    mine = mine + pltpu.roll(mine, 64, 1)
    slots = jnp.concatenate([mine, mine], axis=1)[0:1, :]
    j0, j1 = iota((512, 256), 0), iota((512, 256), 1)
    pick = onehot(
        (lax.div(j0, 8).astype(F32) == slots) & (lax.rem(j0, 8) == lax.div(j1, 32))
    )
    sb[...] = mm(pick, mp[...]).astype(BF16).reshape(NT, 16, 640)
    exch = []
    for o in range(1, NT):
        d = lax.rem(t + o, NT)
        exch.append(remote(sb.at[d], rb.at[t], (z, d)))
    rb[t] = sb[t]

    load_w2.wait()

    def conv_two(k, carry):
        n = 256
        pre = conv_rows(a2, w2, k * n, n, 2 * COLS)
        h = jnp.where(pre > 0, pre, 0.0)
        s = pl.ds(pl.multiple_of(k * n, n), n)
        hf[0, s, :] = h[:, :128]
        hf[1, s, :] = h[:, 128:]
        return carry

    lax.fori_loop(0, 8, conv_two, 0)

    def transpose_two(k, carry):
        s = pl.ds(pl.multiple_of(k * 128, 128), 128)
        a2t[:, s] = a2[s, :].T
        a1e[:, s] = a1[pl.ds(pl.multiple_of(128 + k * 128, 128), 128), :].T
        return carry

    lax.fori_loop(0, 18, transpose_two, 0)

    def transpose_odd(k, carry):
        s = pl.ds(pl.multiple_of(k * 128, 128), 128)
        a1o[:, s] = a1[pl.ds(pl.multiple_of(192 + k * 128, 64), 128), :].T
        return carry

    lax.fori_loop(0, 16, transpose_odd, 0)
    for a in range(3):
        for b in range(3):
            w2t[a, b * CH:(b + 1) * CH, :] = w2[a, (2 - b) * CH:(3 - b) * CH, :].T

    l_rep = onehot(lax.div(iota((256, 32), 0), 8) == iota((256, 32), 1))
    rep = mm(l_rep, lab[...].astype(F32).astype(BF16))
    rep = jnp.where(
        lax.div(iota((256, 64), 1), 8) == lax.rem(iota((256, 64), 0), 8), rep, 0.0
    ).astype(BF16)
    l_sel = onehot(lax.rem(iota((8, 64), 1), 8) == iota((8, 64), 0))
    labels = mm_dims(l_sel, rep, 1, 1)

    for c in exch:
        c.wait_recv()
    got = rb[...].reshape(512, 640)
    from_slot = got[:, 512:640].astype(F32)[:, 24:25]
    n0, n1 = iota((512, 256), 0), iota((512, 256), 1)
    tile_no = (lax.div(n1, 64) * 8 + lax.rem(n1, 8) + 1).astype(F32)
    place = onehot((from_slot == tile_no) & (lax.rem(n0, 8) == lax.rem(lax.div(n1, 8), 8)))
    mean_t[...] = mm_dims(got, place, 0, 0)

    scale = 1.0 / math.sqrt(NZ * NT * CELLS)
    head_w = wh[...]
    classes = iota((NCLS, 256), 0)
    loss = jnp.zeros((1, 256), F32)
    head_t = jnp.zeros((NCLS, CH), F32)
    for b in range(8):
        s = pl.ds(b, 256, stride=8)
        h32 = jnp.concatenate([hf[0, s, :], hf[1, s, :]], axis=1)
        hb = h32.astype(BF16)
        logits = mm_dims(head_w, hb, 0, 1)
        top = jnp.max(logits, axis=0, keepdims=True)
        low = logits - top
        log_s = low - jnp.log(jnp.sum(jnp.exp(low), axis=0, keepdims=True))
        prob = jnp.exp(log_s)
        mean = mean_t[b * 64:(b + 1) * 64, :]
        spr = mean_t[512 + b:513 + b, :] + mean_t[520 + b:521 + b, :] + mean_t[528 + b:529 + b, :]
        wgt = 1.0 / (0.1 + spr)
        hot = classes.astype(F32) == labels[b:b + 1, :]
        ent = jnp.where(mean > 0, mean * jnp.log(jnp.where(mean > 0, mean, 1.0)), 0.0)
        kl = jnp.sum(ent - mean * log_s, axis=0, keepdims=True)
        nll = jnp.sum(jnp.where(hot, log_s, 0.0), axis=0, keepdims=True)
        loss = loss + (wgt * kl - nll)
        lg = ((wgt * (prob - mean) + prob - jnp.where(hot, 1.0, 0.0)) * scale).astype(BF16)
        head_t = head_t + mm(lg, hb)
        hg = mm_dims(lg, head_w, 0, 1)
        g2 = jnp.where(h32 > 0, hg, 0.0)
        gf[0, s, :] = g2[:, :128]
        gf[1, s, :] = g2[:, 128:]

    def round_grad(k, carry):
        s = pl.ds(pl.multiple_of(k * 128, 128), 128)
        d = pl.ds(pl.multiple_of(128 + k * 128, 128), 128)
        gp[d, 0:128] = gf[0, s, :].astype(BF16)
        gp[d, 128:256] = gf[1, s, :].astype(BF16)
        return carry

    lax.fori_loop(0, 16, round_grad, 0)
    gh_up = remote(gp.at[pl.ds(CELLS, 128), :], gp.at[pl.ds(0, 128), :], (z, up))
    gh_dn = remote(gp.at[pl.ds(128, 128), :], gp.at[pl.ds(128 + CELLS, 128), :], (z, down))

    small = {"head": jnp.concatenate([head_t[:, :128], head_t[:, 128:]], axis=0),
             "loss": jnp.broadcast_to(jnp.sum(loss, axis=1, keepdims=True), (8, 128))}

    def small_send(n, axis):
        me = coords[axis]
        hx[n, me] = small["head"].astype(BF16)
        lx[n, me] = small["loss"]
        size = 2 if axis == "c" else 4
        small["wait"] = []
        for o in range(1, size):
            dev = peer(axis, lax.rem(me + o, size))
            small["wait"].append(remote(hx.at[n, me], hx.at[n, me], dev))
            small["wait"].append(remote(lx.at[n, me], lx.at[n, me], dev))

    def small_recv(n, axis):
        for c in small["wait"]:
            c.wait_recv()
        size = 2 if axis == "c" else 4
        h, l = hx[n, 0].astype(F32), lx[n, 0]
        for j in range(1, size):
            h = h + hx[n, j].astype(F32)
            l = l + lx[n, j]
        small["head"], small["loss"] = h, l

    orders = (("x", "y", "z"), ("y", "z", "x"), ("z", "x", "y"))

    class Session:
        def __init__(self, n):
            self.n = n
            self.wait = []

        def done(self):
            for c in self.wait:
                c.wait_recv()
            self.wait = []

        def base(self, p):
            return 768 * p + 192 * coords[orders[p][0]]

        def c_send(self):
            n = self.n
            other = 1 - core

            def step(k, carry):
                s = pl.ds(pl.multiple_of(k * 256, 256), 256)
                csb[n, s, :] = df[n, other, s, :].astype(BF16)
                return carry

            lax.fori_loop(0, 9, step, 0)
            self.wait.append(remote(csb.at[n], crb.at[n], peer("c", other)))

        def s1(self):
            self.done()
            n = self.n

            def step(k, carry):
                s = pl.ds(pl.multiple_of(k * 256, 256), 256)
                v = df[n, core, s, :] + crb[n, s, :].astype(F32)
                acc[n, s, :] = v
                s1b[n, s, :] = v.astype(BF16)
                return carry

            lax.fori_loop(0, 9, step, 0)
            for o in (2, 1, 3):
                for p in range(3):
                    ax = orders[p][0]
                    j = ring(ax, o)
                    src = s1b.at[n, pl.ds(pl.multiple_of(768 * p + 192 * j, 64), 192), :]
                    self.wait.append(remote(src, r1.at[n, p, o], peer(ax, j)))

        def s2(self):
            self.done()
            n = self.n
            for p in range(3):
                s = pl.ds(pl.multiple_of(self.base(p), 64), 192)
                v = acc[n, s, :]
                for o in range(1, 4):
                    v = v + r1[n, p, o].astype(F32)
                a1c[n, p] = v
                s2b[n, p] = v.astype(BF16)
            for o in (2, 1, 3):
                for p in range(3):
                    ax = orders[p][1]
                    j = ring(ax, o)
                    src = s2b.at[n, p, pl.ds(pl.multiple_of(48 * j, 16), 48), :]
                    self.wait.append(remote(src, r2.at[n, p, o], peer(ax, j)))

        def s3(self):
            self.done()
            n = self.n
            for p in range(3):
                s = pl.ds(pl.multiple_of(48 * coords[orders[p][1]], 16), 48)
                v = a1c[n, p, s, :]
                for o in range(1, 4):
                    v = v + r2[n, p, o].astype(F32)
                x3[n, p, coords[orders[p][2]]] = v.astype(BF16)
            for o in (2, 1, 3):
                for p in range(3):
                    ax = orders[p][2]
                    ref = x3.at[n, p, coords[ax]]
                    self.wait.append(remote(ref, ref, peer(ax, ring(ax, o))))

        def g2(self):
            self.done()
            n = self.n
            for p in range(3):
                v = x3[n, p, 0].astype(F32)
                for j in range(1, 4):
                    v = v + x3[n, p, j].astype(F32)
                s = pl.ds(pl.multiple_of(self.base(p) + 48 * coords[orders[p][1]], 16), 48)
                gat[n, core, s, :] = v.astype(BF16)
            for o in (2, 1, 3):
                for p in range(3):
                    ax = orders[p][1]
                    s = pl.ds(pl.multiple_of(self.base(p) + 48 * coords[ax], 16), 48)
                    ref = gat.at[n, core, s, :]
                    self.wait.append(remote(ref, ref, peer(ax, ring(ax, o))))

        def g1(self):
            self.done()
            n = self.n
            for o in (2, 1, 3):
                for p in range(3):
                    ax = orders[p][0]
                    ref = gat.at[n, core, pl.ds(pl.multiple_of(self.base(p), 64), 192), :]
                    self.wait.append(remote(ref, ref, peer(ax, ring(ax, o))))

        def gc(self):
            self.done()
            ref = gat.at[self.n, core]
            self.wait.append(remote(ref, ref, peer("c", 1 - core)))

    second_s, first_s = Session(0), Session(1)

    def kernel_grad(n, a, lhs, rhs):
        d = mm(lhs, rhs)
        df[n, 0, 768 * a:768 * (a + 1), :] = d[:, :128]
        df[n, 1, 768 * a:768 * (a + 1), :] = d[:, 128:]

    small_send(0, "c")
    grad_two = gp[128:128 + CELLS, :]
    for a in range(3):
        kernel_grad(0, a, a2t[:, 128 * a:128 * a + CELLS], grad_two)
    second_s.c_send()
    small_recv(0, "c")
    small_send(1, "x")

    gh_up.wait_recv()
    gh_dn.wait_recv()

    def build_grad(k, carry):
        s = pl.ds(pl.multiple_of(k * 128, 128), 128)
        row = t * ROWS - 2 + 2 * k + lax.div(iota((128, CH), 0), COLS)
        v = jnp.where((row >= 0) & (row < NT * ROWS), gp[s, :].astype(F32), 0.0)
        before, after = shifted(v, 2, 0, 0, 128)
        ag[s, 0:CH] = before
        ag[s, CH:2 * CH] = v.astype(BF16)
        ag[s, 2 * CH:3 * CH] = after
        return carry

    lax.fori_loop(0, 18, build_grad, 0)
    second_s.s1()
    small_recv(1, "x")
    small_send(2, "y")

    def back(k, carry):
        n = 256
        total = None
        for a in range(3):
            s = pl.ds(pl.multiple_of(k * n + (2 - a) * 2 * COLS, 128), n)
            d = mm(ag[s, :], w2t[a])
            total = d if total is None else total + d
        h = a2[pl.ds(pl.multiple_of(128 + k * n, 128), n), CH:2 * CH].astype(F32)
        v = jnp.where(h > 0, total, 0.0).astype(BF16)
        xb[pl.ds(pl.multiple_of(k * n, n), n), :] = v
        return carry

    lax.fori_loop(0, 8, back, 0)
    second_s.s2()
    small_recv(2, "y")
    small_send(3, "z")
    grad_one = xb[0:CELLS, :]
    kernel_grad(1, 0, a1e[:, 0:CELLS], grad_one)
    second_s.s3()
    small_recv(3, "z")
    kernel_grad(1, 1, a1o[...], grad_one)
    kernel_grad(1, 2, a1e[:, 128:128 + CELLS], grad_one)
    first_s.c_send()
    second_s.g2()
    first_s.s1()
    second_s.g1()
    first_s.s2()
    second_s.gc()
    first_s.s3()
    second_s.done()
    outs = []
    for h in range(2):
        c = pltpu.make_async_copy(gat.at[0, h], o2.at[:, pl.ds(128 * h, 128)], lsem.at[7 + h])
        c.start()
        outs.append(c)
    ohead[...] = small["head"]
    oloss[...] = small["loss"]
    first_s.g2()
    first_s.g1()
    first_s.gc()
    first_s.done()
    for h in range(2):
        c = pltpu.make_async_copy(gat.at[1, h], o1.at[:, pl.ds(128 * h, 128)], lsem.at[9 + h])
        c.start()
        outs.append(c)
    for c in sent:
        c.wait_send()
    for c in outs:
        c.wait()


def body(teacher_logits, coverage, features, labels, first_weight, second_weight, head_weight):
    any_spec = pl.BlockSpec(memory_space=pl.ANY)
    vmem = pl.BlockSpec(memory_space=pltpu.VMEM)
    out = [
        jax.ShapeDtypeStruct((2304, 256), BF16),
        jax.ShapeDtypeStruct((2304, 256), BF16),
        jax.ShapeDtypeStruct((128, 128), F32),
        jax.ShapeDtypeStruct((8, 128), F32),
    ]
    V = pltpu.VMEM
    scratch = [
        V((4, 4, 32, 4096), BF16),
        V((2432, CH), BF16),
        V((2432, 3 * CH), BF16),
        V((3 * CH, 2304), BF16),
        V((3 * CH, 2048), BF16),
        V((2304, 3 * CH), BF16),
        V((3 * CH, 2304), BF16),
        V((2304, 3 * CH), BF16),
        V((2304, CH), BF16),
        V((3, 3 * CH, CH), BF16),
        V((3, 3 * CH, CH), BF16),
        V((3, 3 * CH, CH), BF16),
        V((2, CELLS, 128), F32),
        V((2, CELLS, 128), F32),
        V((2, 2, 2304, 128), F32),
        V((2, 2, 2304, 128), BF16),
        V((2, 32, 2048), BF16),
        V((2, 32, 2048), BF16),
        V((2, 2, 32, 2048), BF16),
        V((2, 32, 2048), BF16),
        V((2, 32, 2048), BF16),
        V((2, 32, 2048), F32),
        V((32, 2048), F32),
        V((3, 32, 128), F32),
        V((3, 32, 128), F32),
        V((256, 640), BF16),
        V((NT, 16, 640), BF16),
        V((NT, 16, 640), BF16),
        V((640, 256), F32),
        V((2, 2304, 128), BF16),
        V((2, 2304, 128), BF16),
        V((2, 2304, 128), F32),
        V((2, 2304, 128), BF16),
        V((2, 3, 4, 192, 128), BF16),
        V((2, 3, 192, 128), F32),
        V((2, 3, 192, 128), BF16),
        V((2, 3, 4, 48, 128), BF16),
        V((2, 3, 4, 48, 128), BF16),
        V((4, 4, 128, 128), BF16),
        V((4, 4, 8, 128), F32),
        pltpu.SemaphoreType.DMA((NSEM,)),
        pltpu.SemaphoreType.DMA((NSEM,)),
        pltpu.SemaphoreType.DMA((11,)),
    ]
    first, second, head, loss = pl.pallas_call(
        kernel,
        out_shape=out,
        in_specs=[any_spec, vmem, any_spec, vmem, any_spec, any_spec, vmem],
        out_specs=[any_spec, any_spec, vmem, vmem],
        scratch_shapes=scratch,
        compiler_params=pltpu.CompilerParams(
            collective_id=0, has_side_effects=True, vmem_limit_bytes=67043328
        ),
    )(
        teacher_logits,
        coverage.reshape(1, 128),
        features.reshape(CELLS, CH),
        labels.reshape(ROWS, COLS),
        first_weight.reshape(3, 3 * CH, CH),
        second_weight.reshape(3, 3 * CH, CH),
        head_weight,
    )
    first = first.astype(F32).reshape(3, 3, CH, CH)
    second = second.astype(F32).reshape(3, 3, CH, CH)
    head = jnp.concatenate([head[:64].T, head[64:].T], axis=0)
    return first, second, head, loss[0, 0] / (NZ * NT * CELLS)


def solution(mesh):
    return jax.shard_map(
        body,
        mesh=mesh,
        in_specs=(
            P("member", "tile", None),
            P("tile"),
            P("member", "tile", None, None),
            P("member", "tile", None),
            P(),
            P(),
            P(),
        ),
        out_specs=(P(), P(), P(), P()),
        check_vma=False,
    )
```

profile of v0, /device:TPU:1, one launch (start us, length us, event | category | flops | bytes accessed | tf_op | source)
XLA Modules:
  0.0 119.6 jit_solution(4734019603246458412)
XLA Ops:
  0.6 1.5 %copy.11.wh = bf16[256,64]{1,0:T(8,128)(2,1)} copy(bf16[256,64]{0,1:T(8,128)(2,1)} %param.13) | data formatting | bytes 65536 | tf_op args[6]
  2.1 108.5 %shard_map.102 = (bf16[2304,256]{1,0:T(8,128)(2,1)}, bf16[2304,256]{1,0:T(8,128)(2,1)}, f32[128,128]{1,0:T(8,128)}, f32[8,128]{1,0:T(8,128)}) custom-call(bf16[4,128,4096]{2,1,0:T(8,128)(2,1)} %tl.1, s32[1,128]{1,0:T(1,128)} %bitcast.20, bf16[2048,256]{1,0:T(8,128)(2,1)} %bitcast.18, s32[32,64]{1,0:T(8,128)} %bitcast.19, bf16[3,768,256]{2,1,0:T(8,128)(2,1)} %bitcast.16, ...), custom_call_target="tpu_custom_call" | custom-call | tf_op jit(solution)/shard_map/pallas_call | solution.py:650
  110.6 1.2 slice.11
  112.4 0.8 slice_bitcast_fusion.1
  113.2 0.6 pad_maximum_fusion
  113.9 0.0 copy-start
  113.9 3.0 %convert.3 = f32[3,3,256,256]{3,2,1,0:T(8,128)} convert(bf16[3,3,256,256]{3,2,1,0:T(8,128)(2,1)} %bitcast.15) | non-fusion elementwise | flops 589824 | bytes 3538944 | tf_op jit(solution)/shard_map/reshape | solution.py:669
  116.8 0.0 copy-done
  116.9 1.6 %convert.2 = f32[3,3,256,256]{3,2,1,0:T(8,128)} convert(bf16[3,3,256,256]{3,2,1,0:T(8,128)(2,1)S(1)} %bitcast.14) | non-fusion elementwise | flops 589824 | bytes 3538944 | tf_op jit(solution)/shard_map/reshape | solution.py:668
Async XLA Ops:
  113.9 3.0 %copy-start = (bf16[2304,256]{1,0:T(8,128)(2,1)S(1)}, bf16[2304,256]{1,0:T(8,128)(2,1)}, u32[]{:S(2)}) copy-start(bf16[2304,256]{1,0:T(8,128)(2,1)} %get-tuple-element.8) | copy-start | bytes 3538948
where the time goes:
time: 120 us
  Pallas kernels  108 us (90%)
  other arithmetic  5.25 us (4%)
  local copies, waits for them, and re-layouts  3.46 us (3%)
  between operations  2.42 us (2%)
    pallas_call x1, Pallas kernels, body(): pl.pallas_call(kernel, out_shape=out, in_specs=[any_spec, vmem, any_spec,...  108 us
    reshape x1, other arithmetic, body(): second = second.astype(F32).reshape(3, 3, CH, CH)  2.99 us

commit v1 on v0

v1 whole, which is shorter than its diff:
```python
import math

import jax
import jax.numpy as jnp
from jax import lax
from jax.experimental import pallas as pl
from jax.experimental.pallas import tpu as pltpu
from jax.sharding import PartitionSpec as P

F32 = jnp.float32
BF16 = jnp.bfloat16
I32 = jnp.int32
MESH = pl.DeviceIdType.MESH

CH = 256
NCLS = 64
NZ = 4
NT = 32
ROWS = 32
COLS = 64
CELLS = ROWS * COLS
NSEM = 300
PIECES = (2304, 768, 768, 768)


def iota(shape, dim):
    return lax.broadcasted_iota(I32, shape, dim)


def onehot(mask):
    return jnp.where(mask, 1.0, 0.0).astype(BF16)


def mm(a, b):
    return jnp.dot(a, b, preferred_element_type=F32)


def mm_dims(a, b, ca, cb):
    return lax.dot_general(a, b, (((ca,), (cb,)), ((), ())), preferred_element_type=F32)


def kernel(
    tl, cov, feat, lab, w1h, w2h, wh,
    o1, o2, ohead, oloss,
    tv, xb, a1, a1e, a1o, a2, a2t, ag, gp, w1, w2, w2t, hf, gf, gat,
    rel_s, rel_r, fin_s, fin_l, fin_r, own, part, sec_s, sec_r,
    mp, sb, rb, mean_t, hx, lx, wb, wq, pick_s,
    ssem, rsem, lsem, *piece_refs,
):
    z = lax.axis_index("member")
    t = lax.axis_index("tile")
    core = lax.rem(t, 2)
    xc = lax.rem(lax.div(t, 2), 4)
    yc = lax.div(t, 8)
    coords = {"x": xc, "y": yc, "z": z, "c": core}

    def peer(axis, j):
        if axis == "z":
            return (j, t)
        if axis == "x":
            return (z, yc * 8 + j * 2 + core)
        if axis == "y":
            return (z, j * 8 + xc * 2 + core)
        return (z, yc * 8 + xc * 2 + j)

    used = [0]
    sent = []

    def remote(src, dst, dev):
        i = used[0]
        used[0] += 1
        copy = pltpu.make_async_remote_copy(
            src_ref=src, dst_ref=dst, send_sem=ssem.at[i], recv_sem=rsem.at[i],
            device_id=dev, device_id_type=MESH,
        )
        copy.start()
        sent.append(copy)
        return copy

    def ring(axis, o):
        return lax.rem(coords[axis] + o, 4)

    barrier = pltpu.get_barrier_semaphore()
    for o in range(1, NT):
        pl.semaphore_signal(barrier, inc=1, device_id=(z, lax.rem(t + o, NT)), device_id_type=MESH)
    for o in range(1, NZ):
        pl.semaphore_signal(barrier, inc=1, device_id=(lax.rem(z + o, NZ), t), device_id_type=MESH)

    zr, zl, zf = lax.rem(z + 1, NZ), lax.rem(z + 3, NZ), lax.rem(z + 2, NZ)
    loads = []
    for ci, g in enumerate((zf, zr, zl, z)):
        c = pltpu.make_async_copy(
            tl.at[:, pl.ds(pl.multiple_of(g * 32, 32), 32), :], tv.at[ci], lsem.at[ci]
        )
        c.start()
        loads.append(c)
    load_x = pltpu.make_async_copy(feat, xb.at[pl.ds(192, CELLS), :], lsem.at[4])
    load_w1 = pltpu.make_async_copy(w1h, w1, lsem.at[5])
    load_w2 = pltpu.make_async_copy(w2h, w2, lsem.at[6])
    load_x.start()
    load_w1.start()
    load_w2.start()

    wb[...] = onehot(lax.div(iota((256, 256), 0), 64) == lax.div(iota((256, 256), 1), 64))
    wq[...] = onehot(lax.div(iota((256, 128), 0), 64) == iota((256, 128), 1))

    def cell_sums(v, half, total):
        hi = v.astype(BF16)
        lo = (v - hi.astype(F32)).astype(BF16)
        both = mm(jnp.concatenate([hi, lo], axis=0), wq[...])
        for j in range(8):
            s = both[32 * j:32 * (j + 1)] + both[256 + 32 * j:288 + 32 * j]
            shift = half * 32 + 4 * j
            total = total + (pltpu.roll(s, shift, 1) if shift else s)
        return total

    def soft(ci, half, put, sec):
        x = jnp.concatenate(
            [
                tv[ci, :, :, half * 2048 + 256 * j:half * 2048 + 256 * (j + 1)].reshape(128, 256)
                for j in range(8)
            ],
            axis=0,
        ).astype(F32)
        e4 = jnp.exp2(x * (math.log2(math.e) / 4.0))
        r = e4 / mm(e4.astype(BF16), wb[...])
        r2 = r * r
        e = (r2 * r2).astype(BF16)
        p = e.astype(F32) / mm(e, wb[...])
        p = p.reshape(8, 4, 32, 256)
        sq = p * p
        f = (p[:, 0] + p[:, 1]) + (p[:, 2] + p[:, 3])
        q = (sq[:, 0] + sq[:, 1]) + (sq[:, 2] + sq[:, 3])
        for j in range(8):
            put(j, f[j])
        return cell_sums(q.reshape(256, 256), half, sec)

    def put_to(ref, *lead):
        def put(j, v):
            ref[(*lead, slice(None), slice(256 * j, 256 * (j + 1)))] = v.astype(ref.dtype)

        return put

    zero_sec = jnp.zeros((32, 128), F32)
    loads[0].wait()
    sec_f = soft(0, 0, put_to(rel_s, 0), zero_sec)
    pl.semaphore_wait(barrier, NT - 1 + NZ - 1)
    relay_a = remote(rel_s.at[0], rel_r.at[0], (zr, t))
    up, down = lax.rem(t + 1, NT), lax.rem(t + NT - 1, NT)
    halo_up = remote(feat.at[pl.ds(CELLS - 192, 192), :], xb.at[pl.ds(0, 192), :], (z, up))
    halo_dn = remote(feat.at[pl.ds(0, 192), :], xb.at[pl.ds(192 + CELLS, 192), :], (z, down))
    sec_f = soft(0, 1, put_to(rel_s, 1), sec_f)
    relay_b = remote(rel_s.at[1], rel_r.at[1], (zl, t))
    loads[1].wait()
    sec_1 = soft(1, 1, put_to(fin_s, 0, 1), zero_sec)
    f0 = remote(fin_s.at[0, 1], fin_l.at[1], (zr, t))
    loads[2].wait()
    sec_2 = soft(2, 0, put_to(fin_s, 1, 0), zero_sec)
    f1 = remote(fin_s.at[1, 0], fin_r.at[0], (zl, t))
    sec_1 = soft(1, 0, put_to(part, 0), sec_1)
    sec_2 = soft(2, 1, put_to(part, 1), sec_2)

    def add_relay(side, half):
        fin_s[side, half] = (part[side] + rel_r[half].astype(F32)).astype(BF16)

    relay_a.wait_recv()
    add_relay(0, 0)
    f2 = remote(fin_s.at[0, 0], fin_l.at[0], (zr, t))
    relay_b.wait_recv()
    add_relay(1, 1)
    f3 = remote(fin_s.at[1, 1], fin_r.at[1], (zl, t))
    sec_c = []
    for i, (value, to) in enumerate(((sec_f, zf), (sec_1, zr), (sec_2, zl))):
        sec_s[i] = value
        sec_c.append(remote(sec_s.at[i], sec_r.at[i], (to, t)))
    loads[3].wait()
    sec_m = soft(3, 0, put_to(own, 0), zero_sec)
    sec_m = soft(3, 1, put_to(own, 1), sec_m)

    crow = cov[...]
    i0, i1 = iota((128, 128), 0), iota((128, 128), 1)
    ccol = jnp.sum(jnp.where(i0 == i1, crow, 0), axis=1, keepdims=True)
    same = (ccol == crow) & (lax.div(i0, 32) == lax.div(i1, 32)) & (i0 < i1)
    rank = jnp.sum(jnp.where(same, 1, 0), axis=0, keepdims=True)
    slot = jnp.broadcast_to(crow * 2 + rank, (8, 128)).astype(F32)
    lane8 = iota((8, 128), 1)
    mine = jnp.zeros((8, 128), F32)
    for g in range(NZ):
        moved = slot if g == 0 else pltpu.roll(slot, 128 - 32 * g, 1)
        mine = jnp.where(z == g, moved, mine)
    mine = jnp.where(lane8 < 32, mine, 0.0)
    mine = mine + pltpu.roll(mine, 32, 1)
    mine = mine + pltpu.roll(mine, 64, 1)
    slots = jnp.concatenate([mine, mine], axis=1)[0:1, :]
    j0, j1 = iota((512, 256), 0), iota((512, 256), 1)
    pick_s[...] = onehot(
        (lax.div(j0, 8).astype(F32) == slots) & (lax.rem(j0, 8) == lax.div(j1, 32))
    )

    def shifted(v, by, lo_col, hi_col, rows):
        col = lax.rem(iota((rows, CH), 0), COLS)
        before = jnp.where(col >= by, pltpu.roll(v, by, 0), 0.0)
        after = jnp.where(col < COLS - by, pltpu.roll(v, rows - by, 0), 0.0)
        return before.astype(BF16), after.astype(BF16)

    load_x.wait()
    load_w1.wait()
    halo_up.wait_recv()
    halo_dn.wait_recv()

    def build_one(k, carry):
        s = pl.ds(pl.multiple_of(k * 128, 128), 128)
        row = t * ROWS - 3 + 2 * k + lax.div(iota((128, CH), 0), COLS)
        v = xb[s, :].astype(F32)
        v = jnp.where((row >= 0) & (row < NT * ROWS), v, 0.0)
        before, after = shifted(v, 1, 0, 0, 128)
        a1[s, 0:CH] = before
        a1[s, CH:2 * CH] = v.astype(BF16)
        a1[s, 2 * CH:3 * CH] = after
        return carry

    lax.fori_loop(0, 19, build_one, 0)

    def conv_rows(a_ref, w_ref, start, rows, stride):
        total = None
        for a in range(3):
            s = pl.ds(pl.multiple_of(start + a * stride, 64), rows)
            d = mm(a_ref[s, :], w_ref[a])
            total = d if total is None else total + d
        return total

    def conv_one(k, carry):
        n = 256
        start = k * n
        pre = conv_rows(a1, w1, start, n, COLS)
        row = t * ROWS - 2 + 4 * k + lax.div(iota((n, CH), 0), COLS)
        h = jnp.where((row >= 0) & (row < NT * ROWS) & (pre > 0), pre, 0.0)
        h = h.astype(BF16).astype(F32)
        before, after = shifted(h, 2, 0, 0, n)
        s = pl.ds(pl.multiple_of(start, n), n)
        a2[s, 0:CH] = before
        a2[s, CH:2 * CH] = h.astype(BF16)
        a2[s, 2 * CH:3 * CH] = after
        a1e[:, s] = a1[pl.ds(pl.multiple_of(128 + start, 128), n), :].T
        odd = jnp.minimum(k, 7) * n
        a1o[:, pl.ds(pl.multiple_of(odd, n), n)] = a1[pl.ds(pl.multiple_of(192 + odd, 64), n), :].T
        return carry

    lax.fori_loop(0, 9, conv_one, 0)

    for c in (f0, f1, f2, f3, *sec_c):
        c.wait_recv()

    msq = zero_sec
    for half in range(2):
        m = (
            own[half] + fin_l[half].astype(F32) + fin_r[half].astype(F32)
        ) * (1.0 / 16.0)
        squares = []
        for j in range(8):
            mj = m[:, 256 * j:256 * (j + 1)]
            row = (half * 4 + j // 2) * 32
            mp[row:row + 32, (j % 2) * 256:(j % 2 + 1) * 256] = mj.astype(BF16)
            squares.append(mj * mj)
        msq = cell_sums(jnp.concatenate(squares, axis=0), half, msq)
    second = (sec_m + sec_r[0]) + (sec_r[1] + sec_r[2])
    spread = second * (1.0 / 16.0) - msq
    lane = iota((32, 128), 1)
    slot_no = (iota((32, 128), 0) + 1).astype(F32)
    for a in range(8):
        sp = spread if a == 0 else pltpu.roll(spread, 128 - 8 * a, 1)
        sp = jnp.where(lane < 8, sp, 0.0)
        hi = sp.astype(BF16).astype(F32)
        mid = (sp - hi).astype(BF16).astype(F32)
        lo = sp - hi - mid
        ext = hi + pltpu.roll(mid, 8, 1) + pltpu.roll(lo, 16, 1)
        ext = jnp.where(lane == 24, slot_no, ext)
        mp[a * 32:(a + 1) * 32, 512:640] = ext.astype(BF16)

    sb[...] = mm(pick_s[...], mp[...]).astype(BF16).reshape(NT, 16, 640)
    exch = []
    for o in range(1, NT):
        d = lax.rem(t + o, NT)
        exch.append(remote(sb.at[d], rb.at[t], (z, d)))
    rb[t] = sb[t]

    load_w2.wait()

    def conv_two(k, carry):
        n = 256
        pre = conv_rows(a2, w2, k * n, n, 2 * COLS)
        h = jnp.where(pre > 0, pre, 0.0)
        s = pl.ds(pl.multiple_of(k * n, n), n)
        hf[0, s, :] = h[:, :128]
        hf[1, s, :] = h[:, 128:]
        a2t[:, s] = a2[s, :].T
        return carry

    lax.fori_loop(0, 8, conv_two, 0)
    a2t[:, CELLS:CELLS + 256] = a2[CELLS:CELLS + 256, :].T

    for a in range(3):
        for b in range(3):
            w2t[a, b * CH:(b + 1) * CH, :] = w2[a, (2 - b) * CH:(3 - b) * CH, :].T

    l_rep = onehot(lax.div(iota((256, 32), 0), 8) == iota((256, 32), 1))
    rep = mm(l_rep, lab[...].astype(F32).astype(BF16))
    rep = jnp.where(
        lax.div(iota((256, 64), 1), 8) == lax.rem(iota((256, 64), 0), 8), rep, 0.0
    ).astype(BF16)
    l_sel = onehot(lax.rem(iota((8, 64), 1), 8) == iota((8, 64), 0))
    labels = mm_dims(l_sel, rep, 1, 1)

    for c in exch:
        c.wait_recv()
    got = rb[...].reshape(512, 640)
    from_slot = got[:, 512:640].astype(F32)[:, 24:25]
    n0, n1 = iota((512, 256), 0), iota((512, 256), 1)
    tile_no = (lax.div(n1, 64) * 8 + lax.rem(n1, 8) + 1).astype(F32)
    place = onehot((from_slot == tile_no) & (lax.rem(n0, 8) == lax.rem(lax.div(n1, 8), 8)))
    mean_t[...] = mm_dims(got, place, 0, 0)

    scale = 1.0 / math.sqrt(NZ * NT * CELLS)
    head_w = wh[...]
    classes = iota((NCLS, 256), 0)
    loss = jnp.zeros((1, 256), F32)
    head_t = jnp.zeros((NCLS, CH), F32)
    for b in range(8):
        s = pl.ds(b, 256, stride=8)
        h32 = jnp.concatenate([hf[0, s, :], hf[1, s, :]], axis=1)
        hb = h32.astype(BF16)
        logits = mm_dims(head_w, hb, 1, 1)
        top = jnp.max(logits, axis=0, keepdims=True)
        low = logits - top
        log_s = low - jnp.log(jnp.sum(jnp.exp(low), axis=0, keepdims=True))
        prob = jnp.exp(log_s)
        mean = mean_t[b * 64:(b + 1) * 64, :]
        spr = mean_t[512 + b:513 + b, :] + mean_t[520 + b:521 + b, :] + mean_t[528 + b:529 + b, :]
        wgt = 1.0 / (0.1 + spr)
        hot = classes.astype(F32) == labels[b:b + 1, :]
        ent = jnp.where(mean > 0, mean * jnp.log(jnp.where(mean > 0, mean, 1.0)), 0.0)
        kl = jnp.sum(ent - mean * log_s, axis=0, keepdims=True)
        nll = jnp.sum(jnp.where(hot, log_s, 0.0), axis=0, keepdims=True)
        loss = loss + (wgt * kl - nll)
        lg = ((wgt * (prob - mean) + prob - jnp.where(hot, 1.0, 0.0)) * scale).astype(BF16)
        head_t = head_t + mm(lg, hb)
        hg = mm_dims(lg, head_w, 0, 0)
        g2 = jnp.where(h32 > 0, hg, 0.0)
        gf[0, s, :] = g2[:, :128]
        gf[1, s, :] = g2[:, 128:]

    def round_grad(k, carry):
        s = pl.ds(pl.multiple_of(k * 128, 128), 128)
        d = pl.ds(pl.multiple_of(128 + k * 128, 128), 128)
        gp[d, 0:128] = gf[0, s, :].astype(BF16)
        gp[d, 128:256] = gf[1, s, :].astype(BF16)
        return carry

    lax.fori_loop(0, 16, round_grad, 0)
    gh_up = remote(gp.at[pl.ds(CELLS, 128), :], gp.at[pl.ds(0, 128), :], (z, up))
    gh_dn = remote(gp.at[pl.ds(128, 128), :], gp.at[pl.ds(128 + CELLS, 128), :], (z, down))

    small = {"head": jnp.concatenate([head_t[:, :128], head_t[:, 128:]], axis=0),
             "loss": jnp.broadcast_to(jnp.sum(loss, axis=1, keepdims=True), (8, 128))}

    def small_send(n, axis):
        me = coords[axis]
        hx[n, me] = small["head"].astype(BF16)
        lx[n, me] = small["loss"]
        size = 2 if axis == "c" else 4
        small["wait"] = []
        for o in range(1, size):
            dev = peer(axis, lax.rem(me + o, size))
            small["wait"].append(remote(hx.at[n, me], hx.at[n, me], dev))
            small["wait"].append(remote(lx.at[n, me], lx.at[n, me], dev))

    def small_recv(n, axis):
        for c in small["wait"]:
            c.wait_recv()
        size = 2 if axis == "c" else 4
        h, l = hx[n, 0].astype(F32), lx[n, 0]
        for j in range(1, size):
            h = h + hx[n, j].astype(F32)
            l = l + lx[n, j]
        small["head"], small["loss"] = h, l

    orders = (("x", "y", "z"), ("y", "z", "x"), ("z", "x", "y"))

    class Piece:
        def __init__(self, index):
            self.refs = piece_refs[9 * index:9 * index + 9]
            self.rows = PIECES[index]
            self.n, self.at = (0, 0) if index == 0 else (1, 768 * (index - 1))
            self.wait = []

        def done(self):
            for c in self.wait:
                c.wait_recv()
            self.wait = []

        def spread(self, level, p, j):
            one, two = self.rows // 12, self.rows // 48
            if level == 1:
                return pl.ds(pl.multiple_of(4 * one * p + one * j, 16), one)
            first = one * coords[orders[p][0]]
            return pl.ds(pl.multiple_of(self.at + 4 * one * p + first + two * j, 16), two)

        def product(self, row, lhs, rhs):
            csb, crb, acc = self.refs[:3]
            d = mm(lhs, rhs)
            low, high = d[:, :128], d[:, 128:]
            acc[row:row + 768, :] = jnp.where(core == 0, low, high)
            csb[row:row + 768, :] = jnp.where(core == 0, high, low).astype(BF16)
            s = pl.ds(row, 768)
            self.wait.append(remote(csb.at[s, :], crb.at[s, :], peer("c", 1 - core)))

        def s1(self):
            self.done()
            csb, crb, acc, s1b, r1 = self.refs[:5]

            def step(k, carry):
                s = pl.ds(pl.multiple_of(k * 256, 256), 256)
                v = acc[s, :] + crb[s, :].astype(F32)
                acc[s, :] = v
                s1b[s, :] = v.astype(BF16)
                return carry

            lax.fori_loop(0, self.rows // 256, step, 0)
            for o in (2, 1, 3):
                for p in range(3):
                    ax = orders[p][0]
                    j = ring(ax, o)
                    src = s1b.at[self.spread(1, p, j), :]
                    self.wait.append(remote(src, r1.at[p, o], peer(ax, j)))

        def s2(self):
            self.done()
            acc, r1, a1c, s2b, r2 = self.refs[2], *self.refs[4:8]
            for p in range(3):
                v = acc[self.spread(1, p, coords[orders[p][0]]), :]
                for o in range(1, 4):
                    v = v + r1[p, o].astype(F32)
                a1c[p] = v
                s2b[p] = v.astype(BF16)
            two = self.rows // 48
            for o in (2, 1, 3):
                for p in range(3):
                    ax = orders[p][1]
                    j = ring(ax, o)
                    src = s2b.at[p, pl.ds(pl.multiple_of(two * j, 16), two), :]
                    self.wait.append(remote(src, r2.at[p, o], peer(ax, j)))

        def s3(self):
            self.done()
            a1c, s2b, r2, x3 = self.refs[5:9]
            two = self.rows // 48
            for p in range(3):
                s = pl.ds(pl.multiple_of(two * coords[orders[p][1]], 16), two)
                v = a1c[p, s, :]
                for o in range(1, 4):
                    v = v + r2[p, o].astype(F32)
                x3[p, coords[orders[p][2]]] = v.astype(BF16)
            for o in (2, 1, 3):
                for p in range(3):
                    ax = orders[p][2]
                    ref = x3.at[p, coords[ax]]
                    self.wait.append(remote(ref, ref, peer(ax, ring(ax, o))))

        def g2(self):
            self.done()
            x3 = self.refs[8]
            for p in range(3):
                v = x3[p, 0].astype(F32)
                for j in range(1, 4):
                    v = v + x3[p, j].astype(F32)
                gat[self.n, core, self.spread(2, p, coords[orders[p][1]]), :] = v.astype(BF16)
            for o in (2, 1, 3):
                for p in range(3):
                    ax = orders[p][1]
                    ref = gat.at[self.n, core, self.spread(2, p, coords[ax]), :]
                    self.wait.append(remote(ref, ref, peer(ax, ring(ax, o))))

        def g1(self):
            self.done()
            one = self.rows // 12
            for o in (2, 1, 3):
                for p in range(3):
                    ax = orders[p][0]
                    s = pl.ds(pl.multiple_of(self.at + 4 * one * p + one * coords[ax], 16), one)
                    ref = gat.at[self.n, core, s, :]
                    self.wait.append(remote(ref, ref, peer(ax, ring(ax, o))))

        def gc(self):
            self.done()
            ref = gat.at[self.n, core, pl.ds(self.at, self.rows), :]
            self.wait.append(remote(ref, ref, peer("c", 1 - core)))

        def store(self):
            self.done()
            out = (o2, o1)[self.n]
            s = pl.ds(self.at, self.rows)
            for h in range(2):
                c = pltpu.make_async_copy(
                    gat.at[self.n, h, s, :], out.at[s, pl.ds(128 * h, 128)], lsem.at[7 + len(outs)]
                )
                c.start()
                outs.append(c)

    outs = []
    second = Piece(0)
    firsts = [Piece(1), Piece(2), Piece(3)]

    small_send(0, "c")
    grad_two = gp[128:128 + CELLS, :]
    for a in range(3):
        second.product(768 * a, a2t[:, 128 * a:128 * a + CELLS], grad_two)
    small_recv(0, "c")
    small_send(1, "x")

    gh_up.wait_recv()
    gh_dn.wait_recv()

    def build_grad(k, carry):
        s = pl.ds(pl.multiple_of(k * 128, 128), 128)
        row = t * ROWS - 2 + 2 * k + lax.div(iota((128, CH), 0), COLS)
        v = jnp.where((row >= 0) & (row < NT * ROWS), gp[s, :].astype(F32), 0.0)
        before, after = shifted(v, 2, 0, 0, 128)
        ag[s, 0:CH] = before
        ag[s, CH:2 * CH] = v.astype(BF16)
        ag[s, 2 * CH:3 * CH] = after
        return carry

    lax.fori_loop(0, 18, build_grad, 0)
    second.s1()

    def back(k, carry):
        n = 256
        total = None
        for a in range(3):
            s = pl.ds(pl.multiple_of(k * n + (2 - a) * 2 * COLS, 128), n)
            d = mm(ag[s, :], w2t[a])
            total = d if total is None else total + d
        h = a2[pl.ds(pl.multiple_of(128 + k * n, 128), n), CH:2 * CH].astype(F32)
        v = jnp.where(h > 0, total, 0.0).astype(BF16)
        xb[pl.ds(pl.multiple_of(k * n, n), n), :] = v
        return carry

    lax.fori_loop(0, 4, back, 0)
    small_recv(1, "x")
    small_send(2, "y")
    lax.fori_loop(4, 8, back, 0)
    second.s2()
    grad_one = xb[0:CELLS, :]
    firsts[0].product(0, a1e[:, 0:CELLS], grad_one)
    small_recv(2, "y")
    small_send(3, "z")
    firsts[1].product(0, a1o[...], grad_one)
    firsts[0].s1()
    second.s3()
    firsts[2].product(0, a1e[:, 128:128 + CELLS], grad_one)
    firsts[1].s1()
    firsts[2].s1()
    second.g2()
    small_recv(3, "z")
    for c in firsts:
        c.s2()
    second.g1()
    for c in firsts:
        c.s3()
    second.gc()
    ohead[:, 0:128] = small["head"][:64]
    ohead[:, 128:256] = small["head"][64:]
    oloss[...] = small["loss"]
    for c in firsts:
        c.g2()
    second.store()
    for c in firsts:
        c.g1()
    for c in firsts:
        c.gc()
    for c in firsts:
        c.store()
    for c in sent:
        c.wait_send()
    for c in outs:
        c.wait()


def widen(first, second, head, loss, out_first, out_second, out_head, out_loss):
    out_first[...] = first[...].astype(F32)
    out_second[...] = second[...].astype(F32)
    out_head[...] = head[...]
    out_loss[...] = loss[0:1, 0:1] * (1.0 / (NZ * NT * CELLS))


def body(teacher_logits, coverage, features, labels, first_weight, second_weight, head_weight):
    any_spec = pl.BlockSpec(memory_space=pl.ANY)
    vmem = pl.BlockSpec(memory_space=pltpu.VMEM)
    out = [
        jax.ShapeDtypeStruct((2304, 256), BF16),
        jax.ShapeDtypeStruct((2304, 256), BF16),
        jax.ShapeDtypeStruct((NCLS, CH), F32),
        jax.ShapeDtypeStruct((8, 128), F32),
    ]
    V = pltpu.VMEM
    scratch = [
        V((4, 4, 32, 4096), BF16),
        V((2432, CH), BF16),
        V((2432, 3 * CH), BF16),
        V((3 * CH, 2304), BF16),
        V((3 * CH, 2048), BF16),
        V((2304, 3 * CH), BF16),
        V((3 * CH, 2304), BF16),
        V((2304, 3 * CH), BF16),
        V((2304, CH), BF16),
        V((3, 3 * CH, CH), BF16),
        V((3, 3 * CH, CH), BF16),
        V((3, 3 * CH, CH), BF16),
        V((2, CELLS, 128), F32),
        V((2, CELLS, 128), F32),
        V((2, 2, 2304, 128), BF16),
        V((2, 32, 2048), BF16),
        V((2, 32, 2048), BF16),
        V((2, 2, 32, 2048), BF16),
        V((2, 32, 2048), BF16),
        V((2, 32, 2048), BF16),
        V((2, 32, 2048), F32),
        V((2, 32, 2048), F32),
        V((3, 32, 128), F32),
        V((3, 32, 128), F32),
        V((256, 640), BF16),
        V((NT, 16, 640), BF16),
        V((NT, 16, 640), BF16),
        V((640, 256), F32),
        V((4, 4, 128, 128), BF16),
        V((4, 4, 8, 128), F32),
        V((256, 256), BF16),
        V((256, 128), BF16),
        V((512, 256), BF16),
        pltpu.SemaphoreType.DMA((NSEM,)),
        pltpu.SemaphoreType.DMA((NSEM,)),
        pltpu.SemaphoreType.DMA((16,)),
    ]
    for rows in PIECES:
        scratch += [
            V((rows, 128), BF16),
            V((rows, 128), BF16),
            V((rows, 128), F32),
            V((rows, 128), BF16),
            V((3, 4, rows // 12, 128), BF16),
            V((3, rows // 12, 128), F32),
            V((3, rows // 12, 128), BF16),
            V((3, 4, rows // 48, 128), BF16),
            V((3, 4, rows // 48, 128), BF16),
        ]
    first, second, head, loss = pl.pallas_call(
        kernel,
        out_shape=out,
        in_specs=[any_spec, vmem, any_spec, vmem, any_spec, any_spec, vmem],
        out_specs=[any_spec, any_spec, vmem, vmem],
        scratch_shapes=scratch,
        compiler_params=pltpu.CompilerParams(
            collective_id=0, has_side_effects=True, vmem_limit_bytes=67043328
        ),
    )(
        teacher_logits,
        coverage.reshape(1, 128),
        features.reshape(CELLS, CH),
        labels.reshape(ROWS, COLS),
        first_weight.reshape(3, 3 * CH, CH),
        second_weight.reshape(3, 3 * CH, CH),
        head_weight.T,
    )
    steps, rows = 4, 2304 // 4
    big = pl.BlockSpec((rows, CH), lambda i: (i, 0))
    first, second, head, loss = pl.pallas_call(
        widen,
        grid=(steps,),
        out_shape=[
            jax.ShapeDtypeStruct((2304, CH), F32),
            jax.ShapeDtypeStruct((2304, CH), F32),
            jax.ShapeDtypeStruct((NCLS, CH), F32),
            jax.ShapeDtypeStruct((1, 1), F32),
        ],
        in_specs=[
            big, big, pl.BlockSpec((NCLS, CH), lambda i: (0, 0)), pl.BlockSpec((8, 128), lambda i: (0, 0))
        ],
        out_specs=[
            big, big, pl.BlockSpec((NCLS, CH), lambda i: (0, 0)), pl.BlockSpec((1, 1), lambda i: (0, 0))
        ],
    )(first, second, head, loss)
    return (
        first.reshape(3, 3, CH, CH), second.reshape(3, 3, CH, CH), head.T, loss.reshape(())
    )


def solution(mesh):
    return jax.shard_map(
        body,
        mesh=mesh,
        in_specs=(
            P("member", "tile", None),
            P("tile"),
            P("member", "tile", None, None),
            P("member", "tile", None),
            P(),
            P(),
            P(),
        ),
        out_specs=(P(), P(), P(), P()),
        check_vma=False,
    )
```

time: 120 us -> 85.4 us (0.71)
  Pallas kernels: 108 us -> 84.4 us
  other arithmetic: 5.25 us -> 0 us
  local copies, waits for them, and re-layouts: 3.46 us -> 0 us
  between operations: 2.42 us -> 0.69 us
    pallas_call x1, Pallas kernels: 108 us -> 80.1 us  [body(): pl.pallas_call(kernel, out_shape=out, in_specs=[any_spec, vmem, any_spec,...]
    reshape x2 -> x0, other arithmetic: 4.62 us -> none  [the longest x1 2.99 us: body(): second = second.astype(F32).reshape(3, 3, CH, CH)]
    pallas_call x0 -> x1, Pallas kernels: none -> 4.32 us  [body(): pl.pallas_call(widen, grid=(steps,), out_shape=[jax.ShapeDtypeStruct((230...]
    unnamed x3 -> x0, local copies, waits for them, and re-layouts: 1.5 us -> none
where the time goes in v1:
time: 85.4 us; the launch traced here: 85.1 us
  Pallas kernels  84.4 us (99%)
    pallas_call x1, Pallas kernels, body(): pl.pallas_call(kernel, out_shape=out, in_specs=[any_spec, vmem, any_spec,...  80.1 us
    pallas_call x1, Pallas kernels, body(): pl.pallas_call(widen, grid=(steps,), out_shape=[jax.ShapeDtypeStruct((230...  4.32 us

profile of v1, /device:TPU:1, one launch (start us, length us, event | category | flops | bytes accessed | tf_op | source)
XLA Modules:
  0.0 85.1 jit_solution(17683498522854866611)
XLA Ops:
  0.6 80.1 %shard_map.102 = (bf16[2304,256]{1,0:T(8,128)(2,1)}, bf16[2304,256]{1,0:T(8,128)(2,1)}, f32[64,256]{1,0:T(8,128)}, f32[8,128]{1,0:T(8,128)}) custom-call(bf16[4,128,4096]{2,1,0:T(8,128)(2,1)} %tl.1, s32[1,128]{1,0:T(1,128)} %bitcast.15, bf16[2048,256]{1,0:T(8,128)(2,1)} %bitcast.12, s32[32,64]{1,0:T(8,128)} %bitcast.14, bf16[3,768,256]{2,1,0:T(8,128)(2,1)} %bitcast.10, ...), custom_call_target="tpu_custom_call" | custom-call | tf_op jit(solution)/shard_map/pallas_call | solution.py:656
  80.7 4.3 %shard_map.103 = (f32[2304,256]{1,0:T(8,128)}, f32[2304,256]{1,0:T(8,128)}, f32[64,256]{1,0:T(8,128)}, f32[1,1]{1,0:T(1,128)}) custom-call(bf16[2304,256]{1,0:T(8,128)(2,1)} %get-tuple-element.12.first, bf16[2304,256]{1,0:T(8,128)(2,1)} %get-tuple-element.13.second, f32[64,256]{1,0:T(8,128)} %get-tuple-element.14.head, f32[8,128]{1,0:T(8,128)} %get-tuple-element.15.loss), custom_call_target="tpu_custom_call" | custom-call | tf_op jit(solution)/shard_map/pallas_call | solution.py:676

commit v2 on v1

--- a/solution.py
+++ b/solution.py
@@ -19,7 +19,7 @@
 ROWS = 32
 COLS = 64
 CELLS = ROWS * COLS
-NSEM = 300
+NSEM = 46
 PIECES = (2304, 768, 768, 768)
 
 
@@ -63,19 +63,33 @@
             return (z, j * 8 + xc * 2 + core)
         return (z, yc * 8 + xc * 2 + j)
 
-    used = [0]
-    sent = []
+    groups = []
+
+    class Group:
+        def __init__(self, total):
+            self.total, self.index = total, len(groups)
+            groups.append(self)
+
+        def describe(self, src, dst, dev):
+            return pltpu.make_async_remote_copy(
+                src_ref=src, dst_ref=dst, send_sem=ssem.at[self.index],
+                recv_sem=rsem.at[self.index], device_id=dev, device_id_type=MESH,
+            )
+
+        def send(self, src, dst, dev):
+            self.dev = dev
+            self.describe(src, dst, dev).start()
+
+        def wait_recv(self):
+            self.describe(self.total, self.total, self.dev).wait_recv()
+
+        def wait_send(self):
+            self.describe(self.total, self.total, self.dev).wait_send()
 
     def remote(src, dst, dev):
-        i = used[0]
-        used[0] += 1
-        copy = pltpu.make_async_remote_copy(
-            src_ref=src, dst_ref=dst, send_sem=ssem.at[i], recv_sem=rsem.at[i],
-            device_id=dev, device_id_type=MESH,
-        )
-        copy.start()
-        sent.append(copy)
-        return copy
+        group = Group(dst)
+        group.send(src, dst, dev)
+        return group
 
     def ring(axis, o):
         return lax.rem(coords[axis] + o, 4)
@@ -147,8 +161,9 @@
     pl.semaphore_wait(barrier, NT - 1 + NZ - 1)
     relay_a = remote(rel_s.at[0], rel_r.at[0], (zr, t))
     up, down = lax.rem(t + 1, NT), lax.rem(t + NT - 1, NT)
-    halo_up = remote(feat.at[pl.ds(CELLS - 192, 192), :], xb.at[pl.ds(0, 192), :], (z, up))
-    halo_dn = remote(feat.at[pl.ds(0, 192), :], xb.at[pl.ds(192 + CELLS, 192), :], (z, down))
+    halo = Group(xb.at[pl.ds(0, 384), :])
+    halo.send(feat.at[pl.ds(CELLS - 192, 192), :], xb.at[pl.ds(0, 192), :], (z, up))
+    halo.send(feat.at[pl.ds(0, 192), :], xb.at[pl.ds(192 + CELLS, 192), :], (z, down))
     sec_f = soft(0, 1, put_to(rel_s, 1), sec_f)
     relay_b = remote(rel_s.at[1], rel_r.at[1], (zl, t))
     loads[1].wait()
@@ -169,10 +184,10 @@
     relay_b.wait_recv()
     add_relay(1, 1)
     f3 = remote(fin_s.at[1, 1], fin_r.at[1], (zl, t))
-    sec_c = []
+    sec_c = Group(sec_r)
     for i, (value, to) in enumerate(((sec_f, zf), (sec_1, zr), (sec_2, zl))):
         sec_s[i] = value
-        sec_c.append(remote(sec_s.at[i], sec_r.at[i], (to, t)))
+        sec_c.send(sec_s.at[i], sec_r.at[i], (to, t))
     loads[3].wait()
     sec_m = soft(3, 0, put_to(own, 0), zero_sec)
     sec_m = soft(3, 1, put_to(own, 1), sec_m)
@@ -205,8 +220,7 @@
 
     load_x.wait()
     load_w1.wait()
-    halo_up.wait_recv()
-    halo_dn.wait_recv()
+    halo.wait_recv()
 
     def build_one(k, carry):
         s = pl.ds(pl.multiple_of(k * 128, 128), 128)
@@ -248,7 +262,7 @@
 
     lax.fori_loop(0, 9, conv_one, 0)
 
-    for c in (f0, f1, f2, f3, *sec_c):
+    for c in (f0, f1, f2, f3, sec_c):
         c.wait_recv()
 
     msq = zero_sec
@@ -278,10 +292,10 @@
         mp[a * 32:(a + 1) * 32, 512:640] = ext.astype(BF16)
 
     sb[...] = mm(pick_s[...], mp[...]).astype(BF16).reshape(NT, 16, 640)
-    exch = []
+    exch = Group(rb.at[pl.ds(0, NT - 1)])
     for o in range(1, NT):
         d = lax.rem(t + o, NT)
-        exch.append(remote(sb.at[d], rb.at[t], (z, d)))
+        exch.send(sb.at[d], rb.at[t], (z, d))
     rb[t] = sb[t]
 
     load_w2.wait()
@@ -311,8 +325,7 @@
     l_sel = onehot(lax.rem(iota((8, 64), 1), 8) == iota((8, 64), 0))
     labels = mm_dims(l_sel, rep, 1, 1)
 
-    for c in exch:
-        c.wait_recv()
+    exch.wait_recv()
     got = rb[...].reshape(512, 640)
     from_slot = got[:, 512:640].astype(F32)[:, 24:25]
     n0, n1 = iota((512, 256), 0), iota((512, 256), 1)
@@ -357,8 +370,9 @@
         return carry
 
     lax.fori_loop(0, 16, round_grad, 0)
-    gh_up = remote(gp.at[pl.ds(CELLS, 128), :], gp.at[pl.ds(0, 128), :], (z, up))
-    gh_dn = remote(gp.at[pl.ds(128, 128), :], gp.at[pl.ds(128 + CELLS, 128), :], (z, down))
+    edge = Group(gp.at[pl.ds(0, 256), :])
+    edge.send(gp.at[pl.ds(CELLS, 128), :], gp.at[pl.ds(0, 128), :], (z, up))
+    edge.send(gp.at[pl.ds(128, 128), :], gp.at[pl.ds(128 + CELLS, 128), :], (z, down))
 
     small = {"head": jnp.concatenate([head_t[:, :128], head_t[:, 128:]], axis=0),
              "loss": jnp.broadcast_to(jnp.sum(loss, axis=1, keepdims=True), (8, 128))}
@@ -368,11 +382,12 @@
         hx[n, me] = small["head"].astype(BF16)
         lx[n, me] = small["loss"]
         size = 2 if axis == "c" else 4
-        small["wait"] = []
+        h, l = Group(hx.at[n, pl.ds(1, size - 1)]), Group(lx.at[n, pl.ds(1, size - 1)])
+        small["wait"] = [h, l]
         for o in range(1, size):
             dev = peer(axis, lax.rem(me + o, size))
-            small["wait"].append(remote(hx.at[n, me], hx.at[n, me], dev))
-            small["wait"].append(remote(lx.at[n, me], lx.at[n, me], dev))
+            h.send(hx.at[n, me], hx.at[n, me], dev)
+            l.send(lx.at[n, me], lx.at[n, me], dev)
 
     def small_recv(n, axis):
         for c in small["wait"]:
@@ -391,12 +406,10 @@
             self.refs = piece_refs[9 * index:9 * index + 9]
             self.rows = PIECES[index]
             self.n, self.at = (0, 0) if index == 0 else (1, 768 * (index - 1))
-            self.wait = []
+            self.group = Group(self.refs[1])
 
         def done(self):
-            for c in self.wait:
-                c.wait_recv()
-            self.wait = []
+            self.group.wait_recv()
 
         def spread(self, level, p, j):
             one, two = self.rows // 12, self.rows // 48
@@ -412,7 +425,7 @@
             acc[row:row + 768, :] = jnp.where(core == 0, low, high)
             csb[row:row + 768, :] = jnp.where(core == 0, high, low).astype(BF16)
             s = pl.ds(row, 768)
-            self.wait.append(remote(csb.at[s, :], crb.at[s, :], peer("c", 1 - core)))
+            self.group.send(csb.at[s, :], crb.at[s, :], peer("c", 1 - core))
 
         def s1(self):
             self.done()
@@ -426,12 +439,13 @@
                 return carry
 
             lax.fori_loop(0, self.rows // 256, step, 0)
+            self.group = Group(r1.at[:, pl.ds(1, 3)])
             for o in (2, 1, 3):
                 for p in range(3):
                     ax = orders[p][0]
                     j = ring(ax, o)
                     src = s1b.at[self.spread(1, p, j), :]
-                    self.wait.append(remote(src, r1.at[p, o], peer(ax, j)))
+                    self.group.send(src, r1.at[p, o], peer(ax, j))
 
         def s2(self):
             self.done()
@@ -443,12 +457,13 @@
                 a1c[p] = v
                 s2b[p] = v.astype(BF16)
             two = self.rows // 48
+            self.group = Group(r2.at[:, pl.ds(1, 3)])
             for o in (2, 1, 3):
                 for p in range(3):
                     ax = orders[p][1]
                     j = ring(ax, o)
                     src = s2b.at[p, pl.ds(pl.multiple_of(two * j, 16), two), :]
-                    self.wait.append(remote(src, r2.at[p, o], peer(ax, j)))
+                    self.group.send(src, r2.at[p, o], peer(ax, j))
 
         def s3(self):
             self.done()
@@ -460,11 +475,12 @@
                 for o in range(1, 4):
                     v = v + r2[p, o].astype(F32)
                 x3[p, coords[orders[p][2]]] = v.astype(BF16)
+            self.group = Group(x3.at[:, pl.ds(1, 3)])
             for o in (2, 1, 3):
                 for p in range(3):
                     ax = orders[p][2]
                     ref = x3.at[p, coords[ax]]
-                    self.wait.append(remote(ref, ref, peer(ax, ring(ax, o))))
+                    self.group.send(ref, ref, peer(ax, ring(ax, o)))
 
         def g2(self):
             self.done()
@@ -474,26 +490,28 @@
                 for j in range(1, 4):
                     v = v + x3[p, j].astype(F32)
                 gat[self.n, core, self.spread(2, p, coords[orders[p][1]]), :] = v.astype(BF16)
+            self.group = Group(x3.at[:, pl.ds(1, 3)])
             for o in (2, 1, 3):
                 for p in range(3):
                     ax = orders[p][1]
                     ref = gat.at[self.n, core, self.spread(2, p, coords[ax]), :]
-                    self.wait.append(remote(ref, ref, peer(ax, ring(ax, o))))
+                    self.group.send(ref, ref, peer(ax, ring(ax, o)))
 
         def g1(self):
             self.done()
             one = self.rows // 12
+            self.group = Group(self.refs[4].at[:, pl.ds(1, 3)])
             for o in (2, 1, 3):
                 for p in range(3):
                     ax = orders[p][0]
                     s = pl.ds(pl.multiple_of(self.at + 4 * one * p + one * coords[ax], 16), one)
                     ref = gat.at[self.n, core, s, :]
-                    self.wait.append(remote(ref, ref, peer(ax, ring(ax, o))))
+                    self.group.send(ref, ref, peer(ax, ring(ax, o)))
 
         def gc(self):
             self.done()
             ref = gat.at[self.n, core, pl.ds(self.at, self.rows), :]
-            self.wait.append(remote(ref, ref, peer("c", 1 - core)))
+            self.group = remote(ref, ref, peer("c", 1 - core))
 
         def store(self):
             self.done()
@@ -517,8 +535,7 @@
     small_recv(0, "c")
     small_send(1, "x")
 
-    gh_up.wait_recv()
-    gh_dn.wait_recv()
+    edge.wait_recv()
 
     def build_grad(k, carry):
         s = pl.ds(pl.multiple_of(k * 128, 128), 128)
@@ -556,8 +573,8 @@
     small_send(3, "z")
     firsts[1].product(0, a1o[...], grad_one)
     firsts[0].s1()
+    firsts[2].product(0, a1e[:, 128:128 + CELLS], grad_one)
     second.s3()
-    firsts[2].product(0, a1e[:, 128:128 + CELLS], grad_one)
     firsts[1].s1()
     firsts[2].s1()
     second.g2()
@@ -580,7 +597,7 @@
         c.gc()
     for c in firsts:
         c.store()
-    for c in sent:
+    for c in groups:
         c.wait_send()
     for c in outs:
         c.wait()

time: 85.4 us -> 81.9 us (0.959)
  Pallas kernels: 84.4 us -> 81 us
    pallas_call x1, Pallas kernels: 80.1 us -> 76.7 us  [body(): pl.pallas_call(kernel, out_shape=out, in_specs=[any_spec, vmem, any_spec,...]
where the time goes in v2:
time: 81.9 us; the launch traced here: 81.7 us
  Pallas kernels  81 us (99%)
    pallas_call x1, Pallas kernels, body(): pl.pallas_call(kernel, out_shape=out, in_specs=[any_spec, vmem, any_spec,...  76.7 us
    pallas_call x1, Pallas kernels, body(): pl.pallas_call(widen, grid=(steps,), out_shape=[jax.ShapeDtypeStruct((230...  4.32 us

profile of v2, /device:TPU:1, one launch (start us, length us, event | category | flops | bytes accessed | tf_op | source)
XLA Modules:
  0.0 81.7 jit_solution(9560403376949437512)
XLA Ops:
  0.6 76.7 %shard_map.102 = (bf16[2304,256]{1,0:T(8,128)(2,1)}, bf16[2304,256]{1,0:T(8,128)(2,1)}, f32[64,256]{1,0:T(8,128)}, f32[8,128]{1,0:T(8,128)}) custom-call(bf16[4,128,4096]{2,1,0:T(8,128)(2,1)} %tl.1, s32[1,128]{1,0:T(1,128)} %bitcast.15, bf16[2048,256]{1,0:T(8,128)(2,1)} %bitcast.12, s32[32,64]{1,0:T(8,128)} %bitcast.14, bf16[3,768,256]{2,1,0:T(8,128)(2,1)} %bitcast.10, ...), custom_call_target="tpu_custom_call" | custom-call | tf_op jit(solution)/shard_map/pallas_call | solution.py:673
  77.3 4.3 %shard_map.103 = (f32[2304,256]{1,0:T(8,128)}, f32[2304,256]{1,0:T(8,128)}, f32[64,256]{1,0:T(8,128)}, f32[1,1]{1,0:T(1,128)}) custom-call(bf16[2304,256]{1,0:T(8,128)(2,1)} %get-tuple-element.12.first, bf16[2304,256]{1,0:T(8,128)(2,1)} %get-tuple-element.13.second, f32[64,256]{1,0:T(8,128)} %get-tuple-element.14.head, f32[8,128]{1,0:T(8,128)} %get-tuple-element.15.loss), custom_call_target="tpu_custom_call" | custom-call | tf_op jit(solution)/shard_map/pallas_call | solution.py:693

commit v3 on v2

--- a/solution.py
+++ b/solution.py
@@ -19,7 +19,7 @@
 ROWS = 32
 COLS = 64
 CELLS = ROWS * COLS
-NSEM = 46
+NSEM = 48
 PIECES = (2304, 768, 768, 768)
 
 
@@ -118,17 +118,30 @@
     wb[...] = onehot(lax.div(iota((256, 256), 0), 64) == lax.div(iota((256, 256), 1), 64))
     wq[...] = onehot(lax.div(iota((256, 128), 0), 64) == iota((256, 128), 1))
 
-    def cell_sums(v, half, total):
+    def cell_sums(v):
         hi = v.astype(BF16)
         lo = (v - hi.astype(F32)).astype(BF16)
         both = mm(jnp.concatenate([hi, lo], axis=0), wq[...])
+        total = None
         for j in range(8):
             s = both[32 * j:32 * (j + 1)] + both[256 + 32 * j:288 + 32 * j]
-            shift = half * 32 + 4 * j
-            total = total + (pltpu.roll(s, shift, 1) if shift else s)
+            total = pltpu.roll(s, 4 * j, 1) + total if j else s
         return total
 
-    def soft(ci, half, put, sec):
+    def pack_cells(v):
+        out = v[0:8]
+        for g in range(1, 4):
+            out = out + pltpu.roll(v[8 * g:8 * (g + 1)], 32 * g, 1)
+        return out
+
+    def unpack_cells(v):
+        low = iota((8, 128), 1) < 32
+        return jnp.concatenate(
+            [jnp.where(low, pltpu.roll(v, 128 - 32 * g, 1) if g else v, 0.0) for g in range(4)],
+            axis=0,
+        )
+
+    def soft(ci, half, put):
         x = jnp.concatenate(
             [
                 tv[ci, :, :, half * 2048 + 256 * j:half * 2048 + 256 * (j + 1)].reshape(128, 256)
@@ -147,50 +160,75 @@
         q = (sq[:, 0] + sq[:, 1]) + (sq[:, 2] + sq[:, 3])
         for j in range(8):
             put(j, f[j])
-        return cell_sums(q.reshape(256, 256), half, sec)
-
-    def put_to(ref, *lead):
+        return pack_cells(cell_sums(q.reshape(256, 256)))
+
+    def put_to(*subs):
         def put(j, v):
-            ref[(*lead, slice(None), slice(256 * j, 256 * (j + 1)))] = v.astype(ref.dtype)
+            ref = subs[j // 4]
+            ref[:, 256 * (j % 4):256 * (j % 4 + 1)] = v.astype(ref.dtype)
 
         return put
 
-    zero_sec = jnp.zeros((32, 128), F32)
+    fin = [None, None]
+    relay = [None, None]
+
+    def send_relay(h):
+        relay[h] = (
+            remote(rel_s.at[h, 0], rel_r.at[h, 0], (zr, t)),
+            remote(rel_s.at[h, 1], rel_r.at[h, 1], (zl, t)),
+        )
+        fin[h] = Group(fin_l)
+
+    def send_own(h, side):
+        if side == 0:
+            fin[h].send(fin_s.at[0, h, 1], fin_l.at[h, 1], (zr, t))
+        else:
+            fin[h].send(fin_s.at[1, h, 0], fin_r.at[h, 0], (zl, t))
+
+    def soft_far(h):
+        sec_s[h, 0] = soft(0, h, put_to(rel_s.at[h, 0], rel_s.at[h, 1]))
+
+    def soft_right(h):
+        sec_s[h, 1] = soft(1, h, put_to(part.at[h, 0], fin_s.at[0, h, 1]))
+
+    def soft_left(h):
+        sec_s[h, 2] = soft(2, h, put_to(fin_s.at[1, h, 0], part.at[h, 1]))
+
+    def finish_relay(h):
+        relay[h][0].wait_recv()
+        fin_s[0, h, 0] = (part[h, 0] + rel_r[h, 0].astype(F32)).astype(BF16)
+        fin[h].send(fin_s.at[0, h, 0], fin_l.at[h, 0], (zr, t))
+        relay[h][1].wait_recv()
+        fin_s[1, h, 1] = (part[h, 1] + rel_r[h, 1].astype(F32)).astype(BF16)
+        fin[h].send(fin_s.at[1, h, 1], fin_r.at[h, 1], (zl, t))
+        group = Group(sec_r.at[h])
+        for i, to in enumerate((zf, zr, zl)):
+            group.send(sec_s.at[h, i], sec_r.at[h, i], (to, t))
+        return group
+
     loads[0].wait()
-    sec_f = soft(0, 0, put_to(rel_s, 0), zero_sec)
+    soft_far(0)
     pl.semaphore_wait(barrier, NT - 1 + NZ - 1)
-    relay_a = remote(rel_s.at[0], rel_r.at[0], (zr, t))
+    send_relay(0)
     up, down = lax.rem(t + 1, NT), lax.rem(t + NT - 1, NT)
     halo = Group(xb.at[pl.ds(0, 384), :])
     halo.send(feat.at[pl.ds(CELLS - 192, 192), :], xb.at[pl.ds(0, 192), :], (z, up))
     halo.send(feat.at[pl.ds(0, 192), :], xb.at[pl.ds(192 + CELLS, 192), :], (z, down))
-    sec_f = soft(0, 1, put_to(rel_s, 1), sec_f)
-    relay_b = remote(rel_s.at[1], rel_r.at[1], (zl, t))
     loads[1].wait()
-    sec_1 = soft(1, 1, put_to(fin_s, 0, 1), zero_sec)
-    f0 = remote(fin_s.at[0, 1], fin_l.at[1], (zr, t))
+    soft_right(0)
+    send_own(0, 0)
     loads[2].wait()
-    sec_2 = soft(2, 0, put_to(fin_s, 1, 0), zero_sec)
-    f1 = remote(fin_s.at[1, 0], fin_r.at[0], (zl, t))
-    sec_1 = soft(1, 0, put_to(part, 0), sec_1)
-    sec_2 = soft(2, 1, put_to(part, 1), sec_2)
-
-    def add_relay(side, half):
-        fin_s[side, half] = (part[side] + rel_r[half].astype(F32)).astype(BF16)
-
-    relay_a.wait_recv()
-    add_relay(0, 0)
-    f2 = remote(fin_s.at[0, 0], fin_l.at[0], (zr, t))
-    relay_b.wait_recv()
-    add_relay(1, 1)
-    f3 = remote(fin_s.at[1, 1], fin_r.at[1], (zl, t))
-    sec_c = Group(sec_r)
-    for i, (value, to) in enumerate(((sec_f, zf), (sec_1, zr), (sec_2, zl))):
-        sec_s[i] = value
-        sec_c.send(sec_s.at[i], sec_r.at[i], (to, t))
+    soft_left(0)
+    send_own(0, 1)
+    soft_far(1)
+    soft_right(1)
+    soft_left(1)
+    sec_c = [finish_relay(0), None]
+    send_relay(1)
+    send_own(1, 0)
+    send_own(1, 1)
     loads[3].wait()
-    sec_m = soft(3, 0, put_to(own, 0), zero_sec)
-    sec_m = soft(3, 1, put_to(own, 1), sec_m)
+    sec_m = [soft(3, h, put_to(own.at[h, 0], own.at[h, 1])) for h in range(2)]
 
     crow = cov[...]
     i0, i1 = iota((128, 128), 0), iota((128, 128), 1)
@@ -206,10 +244,10 @@
     mine = jnp.where(lane8 < 32, mine, 0.0)
     mine = mine + pltpu.roll(mine, 32, 1)
     mine = mine + pltpu.roll(mine, 64, 1)
-    slots = jnp.concatenate([mine, mine], axis=1)[0:1, :]
-    j0, j1 = iota((512, 256), 0), iota((512, 256), 1)
+    slots = mine[0:1, :]
+    j0, j1 = iota((256, 128), 0), iota((256, 128), 1)
     pick_s[...] = onehot(
-        (lax.div(j0, 8).astype(F32) == slots) & (lax.rem(j0, 8) == lax.div(j1, 32))
+        (lax.div(j0, 4).astype(F32) == slots) & (lax.rem(j0, 4) == lax.div(j1, 32))
     )
 
     def shifted(v, by, lo_col, hi_col, rows):
@@ -260,43 +298,47 @@
         a1o[:, pl.ds(pl.multiple_of(odd, n), n)] = a1[pl.ds(pl.multiple_of(192 + odd, 64), n), :].T
         return carry
 
-    lax.fori_loop(0, 9, conv_one, 0)
-
-    for c in (f0, f1, f2, f3, sec_c):
-        c.wait_recv()
-
-    msq = zero_sec
-    for half in range(2):
-        m = (
-            own[half] + fin_l[half].astype(F32) + fin_r[half].astype(F32)
-        ) * (1.0 / 16.0)
+    def send_tiles(h):
+        fin[h].wait_recv()
+        sec_c[h].wait_recv()
         squares = []
         for j in range(8):
-            mj = m[:, 256 * j:256 * (j + 1)]
-            row = (half * 4 + j // 2) * 32
-            mp[row:row + 32, (j % 2) * 256:(j % 2 + 1) * 256] = mj.astype(BF16)
-            squares.append(mj * mj)
-        msq = cell_sums(jnp.concatenate(squares, axis=0), half, msq)
-    second = (sec_m + sec_r[0]) + (sec_r[1] + sec_r[2])
-    spread = second * (1.0 / 16.0) - msq
-    lane = iota((32, 128), 1)
-    slot_no = (iota((32, 128), 0) + 1).astype(F32)
-    for a in range(8):
-        sp = spread if a == 0 else pltpu.roll(spread, 128 - 8 * a, 1)
-        sp = jnp.where(lane < 8, sp, 0.0)
-        hi = sp.astype(BF16).astype(F32)
-        mid = (sp - hi).astype(BF16).astype(F32)
-        lo = sp - hi - mid
-        ext = hi + pltpu.roll(mid, 8, 1) + pltpu.roll(lo, 16, 1)
-        ext = jnp.where(lane == 24, slot_no, ext)
-        mp[a * 32:(a + 1) * 32, 512:640] = ext.astype(BF16)
-
-    sb[...] = mm(pick_s[...], mp[...]).astype(BF16).reshape(NT, 16, 640)
-    exch = Group(rb.at[pl.ds(0, NT - 1)])
-    for o in range(1, NT):
-        d = lax.rem(t + o, NT)
-        exch.send(sb.at[d], rb.at[t], (z, d))
-    rb[t] = sb[t]
+            s = slice(256 * (j % 4), 256 * (j % 4 + 1))
+            m = (
+                own[h, j // 4, :, s] + fin_l[h, j // 4, :, s].astype(F32)
+                + fin_r[h, j // 4, :, s].astype(F32)
+            ) * (1.0 / 16.0)
+            row = (j // 2) * 32
+            mp[h, row:row + 32, (j % 2) * 256:(j % 2 + 1) * 256] = m.astype(BF16)
+            squares.append(m * m)
+        msq = cell_sums(jnp.concatenate(squares, axis=0))
+        second = unpack_cells((sec_m[h] + sec_r[h, 0]) + (sec_r[h, 1] + sec_r[h, 2]))
+        spread = second * (1.0 / 16.0) - msq
+        lane = iota((32, 128), 1)
+        slot_no = (iota((32, 128), 0) + 1).astype(F32)
+        for a in range(4):
+            sp = spread if a == 0 else pltpu.roll(spread, 128 - 8 * a, 1)
+            sp = jnp.where(lane < 8, sp, 0.0)
+            hi = sp.astype(BF16).astype(F32)
+            mid = (sp - hi).astype(BF16).astype(F32)
+            lo = sp - hi - mid
+            ext = hi + pltpu.roll(mid, 8, 1) + pltpu.roll(lo, 16, 1)
+            ext = jnp.where(lane == 24, slot_no, ext)
+            mp[h, a * 32:(a + 1) * 32, 512:640] = ext.astype(BF16)
+        sb[h] = mm(pick_s[...], mp[h]).astype(BF16).reshape(NT, 8, 640)
+        group = Group(rb.at[h, pl.ds(0, NT - 1)])
+        for o in range(1, NT):
+            d = lax.rem(t + o, NT)
+            group.send(sb.at[h, d], rb.at[h, t], (z, d))
+        rb[h, t] = sb[h, t]
+        return group
+
+    exch = [send_tiles(0)]
+    sec_c[1] = finish_relay(1)
+    lax.fori_loop(0, 6, conv_one, 0)
+    exch.append(send_tiles(1))
+    lax.fori_loop(6, 9, conv_one, 0)
+
 
     load_w2.wait()
 
@@ -325,12 +367,13 @@
     l_sel = onehot(lax.rem(iota((8, 64), 1), 8) == iota((8, 64), 0))
     labels = mm_dims(l_sel, rep, 1, 1)
 
-    exch.wait_recv()
+    for c in exch:
+        c.wait_recv()
     got = rb[...].reshape(512, 640)
     from_slot = got[:, 512:640].astype(F32)[:, 24:25]
     n0, n1 = iota((512, 256), 0), iota((512, 256), 1)
     tile_no = (lax.div(n1, 64) * 8 + lax.rem(n1, 8) + 1).astype(F32)
-    place = onehot((from_slot == tile_no) & (lax.rem(n0, 8) == lax.rem(lax.div(n1, 8), 8)))
+    place = onehot((from_slot == tile_no) & (lax.div(n0, 256) * 4 + lax.rem(n0, 4) == lax.rem(lax.div(n1, 8), 8)))
     mean_t[...] = mm_dims(got, place, 0, 0)
 
     scale = 1.0 / math.sqrt(NZ * NT * CELLS)
@@ -636,24 +679,24 @@
         V((2, CELLS, 128), F32),
         V((2, CELLS, 128), F32),
         V((2, 2, 2304, 128), BF16),
-        V((2, 32, 2048), BF16),
-        V((2, 32, 2048), BF16),
-        V((2, 2, 32, 2048), BF16),
-        V((2, 32, 2048), BF16),
-        V((2, 32, 2048), BF16),
-        V((2, 32, 2048), F32),
-        V((2, 32, 2048), F32),
-        V((3, 32, 128), F32),
-        V((3, 32, 128), F32),
-        V((256, 640), BF16),
-        V((NT, 16, 640), BF16),
-        V((NT, 16, 640), BF16),
+        V((2, 2, 32, 1024), BF16),
+        V((2, 2, 32, 1024), BF16),
+        V((2, 2, 2, 32, 1024), BF16),
+        V((2, 2, 32, 1024), BF16),
+        V((2, 2, 32, 1024), BF16),
+        V((2, 2, 32, 1024), F32),
+        V((2, 2, 32, 1024), F32),
+        V((2, 3, 8, 128), F32),
+        V((2, 3, 8, 128), F32),
+        V((2, 128, 640), BF16),
+        V((2, NT, 8, 640), BF16),
+        V((2, NT, 8, 640), BF16),
         V((640, 256), F32),
         V((4, 4, 128, 128), BF16),
         V((4, 4, 8, 128), F32),
         V((256, 256), BF16),
         V((256, 128), BF16),
-        V((512, 256), BF16),
+        V((256, 128), BF16),
         pltpu.SemaphoreType.DMA((NSEM,)),
         pltpu.SemaphoreType.DMA((NSEM,)),
         pltpu.SemaphoreType.DMA((16,)),

time: 81.9 us -> 78.8 us (0.962)
  Pallas kernels: 81 us -> 77.8 us
    pallas_call x1, Pallas kernels: 76.7 us -> 73.5 us  [body(): pl.pallas_call(kernel, out_shape=out, in_specs=[any_spec, vmem, any_spec,...]
where the time goes in v3:
time: 78.8 us; the launch traced here: 78.5 us
  Pallas kernels  77.8 us (99%)
    pallas_call x1, Pallas kernels, body(): pl.pallas_call(kernel, out_shape=out, in_specs=[any_spec, vmem, any_spec,...  73.5 us
    pallas_call x1, Pallas kernels, body(): pl.pallas_call(widen, grid=(steps,), out_shape=[jax.ShapeDtypeStruct((230...  4.32 us

profile of v3, /device:TPU:1, one launch (start us, length us, event | category | flops | bytes accessed | tf_op | source)
XLA Modules:
  0.0 78.5 jit_solution(5250178851058582590)
XLA Ops:
  0.6 73.5 %shard_map.102 = (bf16[2304,256]{1,0:T(8,128)(2,1)}, bf16[2304,256]{1,0:T(8,128)(2,1)}, f32[64,256]{1,0:T(8,128)}, f32[8,128]{1,0:T(8,128)}) custom-call(bf16[4,128,4096]{2,1,0:T(8,128)(2,1)} %tl.1, s32[1,128]{1,0:T(1,128)} %bitcast.15, bf16[2048,256]{1,0:T(8,128)(2,1)} %bitcast.12, s32[32,64]{1,0:T(8,128)} %bitcast.14, bf16[3,768,256]{2,1,0:T(8,128)(2,1)} %bitcast.10, ...), custom_call_target="tpu_custom_call" | custom-call | tf_op jit(solution)/shard_map/pallas_call | solution.py:716
  74.2 4.3 %shard_map.103 = (f32[2304,256]{1,0:T(8,128)}, f32[2304,256]{1,0:T(8,128)}, f32[64,256]{1,0:T(8,128)}, f32[1,1]{1,0:T(1,128)}) custom-call(bf16[2304,256]{1,0:T(8,128)(2,1)} %get-tuple-element.12.first, bf16[2304,256]{1,0:T(8,128)(2,1)} %get-tuple-element.13.second, f32[64,256]{1,0:T(8,128)} %get-tuple-element.14.head, f32[8,128]{1,0:T(8,128)} %get-tuple-element.15.loss), custom_call_target="tpu_custom_call" | custom-call | tf_op jit(solution)/shard_map/pallas_call | solution.py:736

commit v4 on v3

--- a/solution.py
+++ b/solution.py
@@ -19,8 +19,8 @@
 ROWS = 32
 COLS = 64
 CELLS = ROWS * COLS
-NSEM = 48
-PIECES = (2304, 768, 768, 768)
+NSEM = 41
+PIECES = (2304, 1536, 768)
 
 
 def iota(shape, dim):
@@ -343,7 +343,7 @@
     load_w2.wait()
 
     def conv_two(k, carry):
-        n = 256
+        n = 512
         pre = conv_rows(a2, w2, k * n, n, 2 * COLS)
         h = jnp.where(pre > 0, pre, 0.0)
         s = pl.ds(pl.multiple_of(k * n, n), n)
@@ -352,7 +352,7 @@
         a2t[:, s] = a2[s, :].T
         return carry
 
-    lax.fori_loop(0, 8, conv_two, 0)
+    lax.fori_loop(0, 4, conv_two, 0)
     a2t[:, CELLS:CELLS + 256] = a2[CELLS:CELLS + 256, :].T
 
     for a in range(3):
@@ -448,7 +448,7 @@
         def __init__(self, index):
             self.refs = piece_refs[9 * index:9 * index + 9]
             self.rows = PIECES[index]
-            self.n, self.at = (0, 0) if index == 0 else (1, 768 * (index - 1))
+            self.n, self.at = ((0, 0), (1, 0), (1, 1536))[index]
             self.group = Group(self.refs[1])
 
         def done(self):
@@ -569,7 +569,7 @@
 
     outs = []
     second = Piece(0)
-    firsts = [Piece(1), Piece(2), Piece(3)]
+    firsts = [Piece(1), Piece(2)]
 
     small_send(0, "c")
     grad_two = gp[128:128 + CELLS, :]
@@ -594,7 +594,7 @@
     second.s1()
 
     def back(k, carry):
-        n = 256
+        n = 512
         total = None
         for a in range(3):
             s = pl.ds(pl.multiple_of(k * n + (2 - a) * 2 * COLS, 128), n)
@@ -605,21 +605,20 @@
         xb[pl.ds(pl.multiple_of(k * n, n), n), :] = v
         return carry
 
-    lax.fori_loop(0, 4, back, 0)
+    lax.fori_loop(0, 2, back, 0)
     small_recv(1, "x")
     small_send(2, "y")
-    lax.fori_loop(4, 8, back, 0)
+    lax.fori_loop(2, 4, back, 0)
     second.s2()
     grad_one = xb[0:CELLS, :]
     firsts[0].product(0, a1e[:, 0:CELLS], grad_one)
     small_recv(2, "y")
     small_send(3, "z")
-    firsts[1].product(0, a1o[...], grad_one)
+    firsts[0].product(768, a1o[...], grad_one)
+    firsts[1].product(0, a1e[:, 128:128 + CELLS], grad_one)
+    second.s3()
     firsts[0].s1()
-    firsts[2].product(0, a1e[:, 128:128 + CELLS], grad_one)
-    second.s3()
     firsts[1].s1()
-    firsts[2].s1()
     second.g2()
     small_recv(3, "z")
     for c in firsts:
@@ -627,12 +626,12 @@
     second.g1()
     for c in firsts:
         c.s3()
-    second.gc()
     ohead[:, 0:128] = small["head"][:64]
     ohead[:, 128:256] = small["head"][64:]
     oloss[...] = small["loss"]
     for c in firsts:
         c.g2()
+    second.gc()
     second.store()
     for c in firsts:
         c.g1()

time: 78.8 us -> 78.7 us (level)
  no operation moved by 1% of the time
where the time goes in v4:
time: 78.7 us; the launch traced here: 78.5 us
  Pallas kernels  77.8 us (99%)
    pallas_call x1, Pallas kernels, body(): pl.pallas_call(kernel, out_shape=out, in_specs=[any_spec, vmem, any_spec,...  73.5 us
    pallas_call x1, Pallas kernels, body(): pl.pallas_call(widen, grid=(steps,), out_shape=[jax.ShapeDtypeStruct((230...  4.32 us

profile of v4, /device:TPU:1, one launch (start us, length us, event | category | flops | bytes accessed | tf_op | source)
XLA Modules:
  0.0 78.5 jit_solution(1267015693984984547)
XLA Ops:
  0.6 73.5 %shard_map.102 = (bf16[2304,256]{1,0:T(8,128)(2,1)}, bf16[2304,256]{1,0:T(8,128)(2,1)}, f32[64,256]{1,0:T(8,128)}, f32[8,128]{1,0:T(8,128)}) custom-call(bf16[4,128,4096]{2,1,0:T(8,128)(2,1)} %tl.1, s32[1,128]{1,0:T(1,128)} %bitcast.15, bf16[2048,256]{1,0:T(8,128)(2,1)} %bitcast.12, s32[32,64]{1,0:T(8,128)} %bitcast.14, bf16[3,768,256]{2,1,0:T(8,128)(2,1)} %bitcast.10, ...), custom_call_target="tpu_custom_call" | custom-call | tf_op jit(solution)/shard_map/pallas_call | solution.py:715
  74.1 4.3 %shard_map.103 = (f32[2304,256]{1,0:T(8,128)}, f32[2304,256]{1,0:T(8,128)}, f32[64,256]{1,0:T(8,128)}, f32[1,1]{1,0:T(1,128)}) custom-call(bf16[2304,256]{1,0:T(8,128)(2,1)} %get-tuple-element.12.first, bf16[2304,256]{1,0:T(8,128)(2,1)} %get-tuple-element.13.second, f32[64,256]{1,0:T(8,128)} %get-tuple-element.14.head, f32[8,128]{1,0:T(8,128)} %get-tuple-element.15.loss), custom_call_target="tpu_custom_call" | custom-call | tf_op jit(solution)/shard_map/pallas_call | solution.py:735

commit v5 on v3

--- a/solution.py
+++ b/solution.py
@@ -40,11 +40,12 @@
 
 
 def kernel(
-    tl, cov, feat, lab, w1h, w2h, wh,
+    tl, cov_h, feat, lab_h, w1h, w2h, wh_h,
     o1, o2, ohead, oloss,
     tv, xb, a1, a1e, a1o, a2, a2t, ag, gp, w1, w2, w2t, hf, gf, gat,
     rel_s, rel_r, fin_s, fin_l, fin_r, own, part, sec_s, sec_r,
     mp, sb, rb, mean_t, hx, lx, wb, wq, pick_s,
+    cov, lab, wh, head_v, loss_v,
     ssem, rsem, lsem, *piece_refs,
 ):
     z = lax.axis_index("member")
@@ -114,6 +115,12 @@
     load_x.start()
     load_w1.start()
     load_w2.start()
+    load_small = [
+        pltpu.make_async_copy(a, b, lsem.at[16 + i])
+        for i, (a, b) in enumerate(((cov_h, cov), (lab_h, lab), (wh_h, wh)))
+    ]
+    for c in load_small:
+        c.start()
 
     wb[...] = onehot(lax.div(iota((256, 256), 0), 64) == lax.div(iota((256, 256), 1), 64))
     wq[...] = onehot(lax.div(iota((256, 128), 0), 64) == iota((256, 128), 1))
@@ -230,6 +237,8 @@
     loads[3].wait()
     sec_m = [soft(3, h, put_to(own.at[h, 0], own.at[h, 1])) for h in range(2)]
 
+    for c in load_small:
+        c.wait()
     crow = cov[...]
     i0, i1 = iota((128, 128), 0), iota((128, 128), 1)
     ccol = jnp.sum(jnp.where(i0 == i1, crow, 0), axis=1, keepdims=True)
@@ -567,7 +576,7 @@
                 c.start()
                 outs.append(c)
 
-    outs = []
+    outs, late = [], []
     second = Piece(0)
     firsts = [Piece(1), Piece(2), Piece(3)]
 
@@ -605,44 +614,47 @@
         xb[pl.ds(pl.multiple_of(k * n, n), n), :] = v
         return carry
 
-    lax.fori_loop(0, 4, back, 0)
-    small_recv(1, "x")
-    small_send(2, "y")
-    lax.fori_loop(4, 8, back, 0)
+    lax.fori_loop(0, 8, back, 0)
     second.s2()
     grad_one = xb[0:CELLS, :]
     firsts[0].product(0, a1e[:, 0:CELLS], grad_one)
-    small_recv(2, "y")
-    small_send(3, "z")
     firsts[1].product(0, a1o[...], grad_one)
     firsts[0].s1()
     firsts[2].product(0, a1e[:, 128:128 + CELLS], grad_one)
     second.s3()
     firsts[1].s1()
     firsts[2].s1()
+    small_recv(1, "x")
+    small_send(2, "y")
     second.g2()
-    small_recv(3, "z")
     for c in firsts:
         c.s2()
+    small_recv(2, "y")
+    small_send(3, "z")
     second.g1()
     for c in firsts:
         c.s3()
-    second.gc()
-    ohead[:, 0:128] = small["head"][:64]
-    ohead[:, 128:256] = small["head"][64:]
-    oloss[...] = small["loss"]
+    small_recv(3, "z")
+    head_v[:, 0:128] = small["head"][:64]
+    head_v[:, 128:256] = small["head"][64:]
+    loss_v[...] = small["loss"]
+    for i, (a, b) in enumerate(((head_v, ohead), (loss_v, oloss))):
+        c = pltpu.make_async_copy(a, b, lsem.at[19 + i])
+        c.start()
+        late.append(c)
     for c in firsts:
         c.g2()
-    second.store()
+    second.gc()
     for c in firsts:
         c.g1()
+    second.store()
     for c in firsts:
         c.gc()
     for c in firsts:
         c.store()
     for c in groups:
         c.wait_send()
-    for c in outs:
+    for c in outs + late:
         c.wait()
 
 
@@ -655,7 +667,6 @@
 
 def body(teacher_logits, coverage, features, labels, first_weight, second_weight, head_weight):
     any_spec = pl.BlockSpec(memory_space=pl.ANY)
-    vmem = pl.BlockSpec(memory_space=pltpu.VMEM)
     out = [
         jax.ShapeDtypeStruct((2304, 256), BF16),
         jax.ShapeDtypeStruct((2304, 256), BF16),
@@ -697,9 +708,14 @@
         V((256, 256), BF16),
         V((256, 128), BF16),
         V((256, 128), BF16),
+        V((1, 128), I32),
+        V((ROWS, COLS), I32),
+        V((NCLS, CH), BF16),
+        V((NCLS, CH), F32),
+        V((8, 128), F32),
         pltpu.SemaphoreType.DMA((NSEM,)),
         pltpu.SemaphoreType.DMA((NSEM,)),
-        pltpu.SemaphoreType.DMA((16,)),
+        pltpu.SemaphoreType.DMA((21,)),
     ]
     for rows in PIECES:
         scratch += [
@@ -716,8 +732,8 @@
     first, second, head, loss = pl.pallas_call(
         kernel,
         out_shape=out,
-        in_specs=[any_spec, vmem, any_spec, vmem, any_spec, any_spec, vmem],
-        out_specs=[any_spec, any_spec, vmem, vmem],
+        in_specs=[any_spec] * 7,
+        out_specs=[any_spec] * 4,
         scratch_shapes=scratch,
         compiler_params=pltpu.CompilerParams(
             collective_id=0, has_side_effects=True, vmem_limit_bytes=67043328

time: 78.8 us -> 77.1 us (0.978)
  Pallas kernels: 77.8 us -> 76.2 us
    pallas_call x1, Pallas kernels: 73.5 us -> 71.9 us  [body(): pl.pallas_call(kernel, out_shape=out, in_specs=[any_spec] * 7, out_specs=...]
where the time goes in v5:
time: 77.1 us; the launch traced here: 76.9 us
  Pallas kernels  76.2 us (99%)
    pallas_call x1, Pallas kernels, body(): pl.pallas_call(kernel, out_shape=out, in_specs=[any_spec] * 7, out_specs=...  71.9 us
    pallas_call x1, Pallas kernels, body(): pl.pallas_call(widen, grid=(steps,), out_shape=[jax.ShapeDtypeStruct((230...  4.32 us

profile of v5, /device:TPU:1, one launch (start us, length us, event | category | flops | bytes accessed | tf_op | source)
XLA Modules:
  0.0 76.9 jit_solution(15416987291610474481)
XLA Ops:
  0.6 71.9 %shard_map.102 = (bf16[2304,256]{1,0:T(8,128)(2,1)}, bf16[2304,256]{1,0:T(8,128)(2,1)}, f32[64,256]{1,0:T(8,128)}, f32[8,128]{1,0:T(8,128)}) custom-call(bf16[4,128,4096]{2,1,0:T(8,128)(2,1)} %tl.1, s32[1,128]{1,0:T(1,128)} %bitcast.15, bf16[2048,256]{1,0:T(8,128)(2,1)} %bitcast.12, s32[32,64]{1,0:T(8,128)} %bitcast.14, bf16[3,768,256]{2,1,0:T(8,128)(2,1)} %bitcast.10, ...), custom_call_target="tpu_custom_call" | custom-call | tf_op jit(solution)/shard_map/pallas_call | solution.py:732
  72.5 4.3 %shard_map.103 = (f32[2304,256]{1,0:T(8,128)}, f32[2304,256]{1,0:T(8,128)}, f32[64,256]{1,0:T(8,128)}, f32[1,1]{1,0:T(1,128)}) custom-call(bf16[2304,256]{1,0:T(8,128)(2,1)} %get-tuple-element.12.first, bf16[2304,256]{1,0:T(8,128)(2,1)} %get-tuple-element.13.second, f32[64,256]{1,0:T(8,128)} %get-tuple-element.14.head, f32[8,128]{1,0:T(8,128)} %get-tuple-element.15.loss), custom_call_target="tpu_custom_call" | custom-call | tf_op jit(solution)/shard_map/pallas_call | solution.py:752

commit v6 on v5

--- a/solution.py
+++ b/solution.py
@@ -658,11 +658,36 @@
         c.wait()
 
 
-def widen(first, second, head, loss, out_first, out_second, out_head, out_loss):
-    out_first[...] = first[...].astype(F32)
-    out_second[...] = second[...].astype(F32)
-    out_head[...] = head[...]
-    out_loss[...] = loss[0:1, 0:1] * (1.0 / (NZ * NT * CELLS))
+def widen(first, second, head, loss, out_first, out_second, out_head, out_loss,
+          narrow, wide, head_v, loss_v, sem_in, sem_out):
+    rows = 2304 // 4
+    reads, writes = [], []
+    for i in range(8):
+        s = pl.ds(rows * (i // 2), rows)
+        reads.append(
+            pltpu.make_async_copy((first, second)[i % 2].at[s, :], narrow.at[i % 2, s, :], sem_in.at[i])
+        )
+        writes.append(
+            pltpu.make_async_copy(
+                wide.at[i % 2, s, :], (out_first, out_second)[i % 2].at[s, :], sem_out.at[i]
+            )
+        )
+    read_loss = pltpu.make_async_copy(loss, loss_v, sem_in.at[8])
+    read_head = pltpu.make_async_copy(head, head_v, sem_in.at[9])
+    write_head = pltpu.make_async_copy(head_v, out_head, sem_out.at[8])
+    for c in (*reads, read_loss, read_head):
+        c.start()
+    for i in range(8):
+        s = pl.ds(rows * (i // 2), rows)
+        reads[i].wait()
+        wide[i % 2, s, :] = narrow[i % 2, s, :].astype(F32)
+        writes[i].start()
+    read_head.wait()
+    write_head.start()
+    read_loss.wait()
+    out_loss[...] = loss_v[0:1, 0:1] * (1.0 / (NZ * NT * CELLS))
+    for c in (*writes, write_head):
+        c.wait()
 
 
 def body(teacher_logits, coverage, features, labels, first_weight, second_weight, head_weight):
@@ -747,22 +772,23 @@
         second_weight.reshape(3, 3 * CH, CH),
         head_weight.T,
     )
-    steps, rows = 4, 2304 // 4
-    big = pl.BlockSpec((rows, CH), lambda i: (i, 0))
     first, second, head, loss = pl.pallas_call(
         widen,
-        grid=(steps,),
         out_shape=[
             jax.ShapeDtypeStruct((2304, CH), F32),
             jax.ShapeDtypeStruct((2304, CH), F32),
             jax.ShapeDtypeStruct((NCLS, CH), F32),
             jax.ShapeDtypeStruct((1, 1), F32),
         ],
-        in_specs=[
-            big, big, pl.BlockSpec((NCLS, CH), lambda i: (0, 0)), pl.BlockSpec((8, 128), lambda i: (0, 0))
-        ],
-        out_specs=[
-            big, big, pl.BlockSpec((NCLS, CH), lambda i: (0, 0)), pl.BlockSpec((1, 1), lambda i: (0, 0))
+        in_specs=[any_spec] * 4,
+        out_specs=[any_spec] * 3 + [pl.BlockSpec(memory_space=pltpu.VMEM)],
+        scratch_shapes=[
+            V((2, 2304, CH), BF16),
+            V((2, 2304, CH), F32),
+            V((NCLS, CH), F32),
+            V((8, 128), F32),
+            pltpu.SemaphoreType.DMA((10,)),
+            pltpu.SemaphoreType.DMA((9,)),
         ],
     )(first, second, head, loss)
     return (

time: 77.1 us -> 76.7 us (level)
  no operation moved by 1% of the time
where the time goes in v6:
time: 76.7 us; the launch traced here: 76.6 us
  Pallas kernels  75.8 us (99%)
  between operations  0.8 us (1%)
    pallas_call x1, Pallas kernels, body(): pl.pallas_call(kernel, out_shape=out, in_specs=[any_spec] * 7, out_specs=...  71.9 us
    pallas_call x1, Pallas kernels, body(): pl.pallas_call(widen, out_shape=[jax.ShapeDtypeStruct((2304, CH), F32), j...  3.86 us

profile of v6, /device:TPU:1, one launch (start us, length us, event | category | flops | bytes accessed | tf_op | source)
XLA Modules:
  0.0 76.6 jit_solution(365635420351341933)
XLA Ops:
  0.6 71.9 %shard_map.102 = (bf16[2304,256]{1,0:T(8,128)(2,1)}, bf16[2304,256]{1,0:T(8,128)(2,1)}, f32[64,256]{1,0:T(8,128)}, f32[8,128]{1,0:T(8,128)}) custom-call(bf16[4,128,4096]{2,1,0:T(8,128)(2,1)} %tl.1, s32[1,128]{1,0:T(1,128)} %bitcast.15, bf16[2048,256]{1,0:T(8,128)(2,1)} %bitcast.12, s32[32,64]{1,0:T(8,128)} %bitcast.14, bf16[3,768,256]{2,1,0:T(8,128)(2,1)} %bitcast.10, ...), custom_call_target="tpu_custom_call" | custom-call | tf_op jit(solution)/shard_map/pallas_call | solution.py:757
  72.5 3.9 %shard_map.103 = (f32[2304,256]{1,0:T(8,128)}, f32[2304,256]{1,0:T(8,128)}, f32[64,256]{1,0:T(8,128)}, f32[1,1]{1,0:T(1,128)}) custom-call(bf16[2304,256]{1,0:T(8,128)(2,1)} %get-tuple-element.12.first, bf16[2304,256]{1,0:T(8,128)(2,1)} %get-tuple-element.13.second, f32[64,256]{1,0:T(8,128)} %get-tuple-element.14.head, f32[8,128]{1,0:T(8,128)} %get-tuple-element.15.loss), custom_call_target="tpu_custom_call" | custom-call | tf_op jit(solution)/shard_map/pallas_call | solution.py:775
